TPU v7x, 32 devices: a whole 2x2x4 slice. The times are simulated.
32 devices in a mesh: replica: 8 (over y, x, core), shard: 4 (over z).
Axes of the slice: x: 2, y: 2, z: 4, core: 2. Of those that a mesh axis runs over, the one named last changes fastest.
Arguments:
- tokens: bfloat16 [64, 197, 768], P(('replica', 'shard')), may hold values from -6 to 6
- expert_ids: int32 [64, 197, 2], P(('replica', 'shard')), may hold values from 0 to 3, all different within a row; in each aligned block of 394 rows (0 to 393, 394 to 787, ..., all dimensions but the last counted through in order) at most 264 rows name the same one
- qkv_weight: bfloat16 [3, 768, 2304], P(None, 'shard'), may hold values from -0.21875 to 0.21875
- out_weight: bfloat16 [3, 768, 768], P(None, 'shard'), may hold values from -0.875 to 0.875
- router_weight: bfloat16 [3, 768, 4], P(None, 'shard'), may hold values from -0.21875 to 0.21875
- norm_gain: float32 [3, 2, 768], replicated, may hold values from 0.5 to 1.5
- norm_shift: float32 [3, 2, 768], replicated, may hold values from -2 to 2
- expert_in: bfloat16 [3, 4, 768, 3072], P(None, 'shard'), may hold values from -0.21875 to 0.21875
- expert_out: bfloat16 [3, 4, 3072, 768], P(None, 'shard'), may hold values from -0.625 to 0.625
- cotangent: bfloat16 [64, 197, 768], P(('replica', 'shard')), may hold values from -6 to 6
Outputs:
- activations: bfloat16 [64, 197, 768], P(('replica', 'shard'))
- input_grad: float32 [64, 197, 768], P(('replica', 'shard'))
- qkv_grad: float32 [3, 768, 2304], P(None, 'shard')
- out_grad: float32 [3, 768, 768], P(None, 'shard')
- router_grad: float32 [3, 768, 4], P(None, 'shard')
- gain_grad: float32 [3, 2, 768], P(None, None, 'shard')
- shift_grad: float32 [3, 2, 768], P(None, None, 'shard')
- expert_in_grad: float32 [3, 4, 768, 3072], P(None, 'shard', None, 'replica')
- expert_out_grad: float32 [3, 4, 3072, 768], P(None, 'shard', 'replica')
Inputs may be any that keep to these rules, and one draw needn't show every extreme that they name: `expert_ids`: the two ids of a token differ. Among the 394 tokens of one device no expert is named more than 264 times, and in every draw some device names some expert exactly 264 times.
All inputs are finite; a program needn't handle non-finite values.
Results may differ from a plain program's by a relative error of at most 0.025.
Values may be sent and summed in bfloat16 or wider, within the bound.
No kernel may reach another device: no remote copies, remote signals or barrier semaphores. Data moves between devices by JAX's collectives and lax.ppermute only.
A program may use at most 384 MiB of HBM per device.

v0:
```python
import functools

import jax
import jax.numpy as jnp
from jax import lax
from jax.experimental import pallas as pl
from jax.experimental.pallas import tpu as pltpu
from jax.sharding import PartitionSpec as P


HEAD = 64
LAYERS = 3

eps_norm = 1e-06
inv_root_two = 0.7071067811865476
inv_root_two_pi = 0.3989422804014327
bf16 = jnp.bfloat16
f32 = jnp.float32


def dot_on(left, right, left_axis, right_axis):
    return lax.dot_general(
        left, right, (((left_axis,), (right_axis,)), ((), ())), preferred_element_type=f32
    )


def swap(values, axis, bit):
    count = lax.axis_size(axis)
    return lax.ppermute(values, axis, [(n, n ^ bit) for n in range(count)])


def bit_of(axis, bit):
    return (lax.axis_index(axis) & bit) != 0


def bits_from(axis, step):
    bits = []
    while step < lax.axis_size(axis):
        bits.append(step)
        step *= 2
    return bits


def orders():
    bits = bits_from("replica", 2)
    return bits, bits[::-1]


def add_swapped(values, axis, bit, size, at):
    lead, rows, rest = values.shape[:at], values.shape[at], values.shape[at + 1 :]
    view = values.reshape(lead + (rows // (2 * size), 2, size) + rest)
    own = bit_of(axis, bit).astype(jnp.int32)
    kept = lax.dynamic_index_in_dim(view, own, at + 1, keepdims=False)
    sent = lax.dynamic_index_in_dim(view, 1 - own, at + 1, keepdims=False)
    shape = lead + (rows // 2,) + rest
    arrived = swap(sent.reshape(shape), axis, bit)
    return (kept.reshape(shape).astype(f32) + arrived.astype(f32)).astype(bf16)


def join_swapped(values, axis, bit, size, at):
    other = swap(values, axis, bit)
    lead, rows, rest = values.shape[:at], values.shape[at], values.shape[at + 1 :]
    shape = lead + (rows // size, size) + rest
    mine, theirs = values.reshape(shape), other.reshape(shape)
    upper = bit_of(axis, bit)
    pair = [jnp.where(upper, theirs, mine), jnp.where(upper, mine, theirs)]
    return jnp.stack(pair, axis=at + 1).reshape(lead + (2 * rows,) + rest)


def size_below(bit, held):
    size = 1
    for other in held:
        if other < bit:
            size *= 2
    return size


def cut(values):
    middle = values.shape[-2] // 16 * 8
    return (values[..., :middle, :], values[..., middle:, :])


def scatter_replica(values, *others):
    values = add_swapped(values, "replica", 1, 1, 1)
    values, *others = lax.optimization_barrier((values,) + others)
    parts = []
    for piece, order in zip(cut(values), orders()):
        for at, bit in enumerate(order):
            piece = add_swapped(piece, "replica", bit, size_below(bit, order[at + 1 :]), 1)
        parts.append(piece[:, 0])
    return jnp.concatenate(parts, axis=-2), others


def gather_replica(values):
    done = []
    for piece, order in zip(cut(values), orders()):
        piece = piece[:, None]
        held = []
        for bit in order[::-1]:
            piece = join_swapped(piece, "replica", bit, size_below(bit, held), 1)
            held.append(bit)
        done.append(piece)
    return join_swapped(jnp.concatenate(done, axis=-2), "replica", 1, 1, 1)


def after(values, *others):
    return lax.optimization_barrier((values,) + others)[0]


def gather_shard(packed):
    rows, columns = packed.shape
    width = columns // lax.axis_size("replica")
    own = lax.dynamic_slice_in_dim(packed, lax.axis_index("replica") * width, width, axis=1)
    shards_ = lax.axis_size("shard")
    spread = jnp.broadcast_to(own[None], (shards_, rows, width))
    tall = lax.all_to_all(spread, "shard", split_axis=0, concat_axis=0, tiled=True)
    return tall.reshape(shards_ * rows, width)


def split_sum(summed, features):
    if isinstance(summed, tuple):
        return summed
    return summed[:, :features], summed[:, features:]


def norm_rows_of(values, features):
    average = jnp.sum(values, axis=-1, keepdims=True) * (1.0 / features)
    centred = values - average
    variance = jnp.sum(centred * centred, axis=-1, keepdims=True) * (1.0 / features)
    inverse = lax.rsqrt(variance + eps_norm)
    return centred * inverse, inverse


def soft_scores(queries, key_rows, length):
    scores = dot_on(queries, key_rows, 1, 1) * HEAD ** (-0.5)
    column = lax.broadcasted_iota(jnp.int32, scores.shape, 1)
    scores = jnp.where(column < length, scores, -1e30)
    raised = jnp.exp(scores - jnp.max(scores, axis=-1, keepdims=True))
    return raised * (1.0 / jnp.sum(raised, axis=-1, keepdims=True))


def attention_kernel(length, res_ref, w_ref, rt_ref, gain_ref, shift_ref, qkv_ref, ctx_ref, mid_ref, hid_ref, log_ref):
    residual = res_ref[0]
    features = residual.shape[1]
    normed, _ = norm_rows_of(residual, features)
    hidden = (normed * gain_ref[0:1] + shift_ref[0:1]).astype(bf16)
    width = w_ref.shape[2]
    inner = 3 * features // width
    for chunk in range(inner):
        qkv_ref[0, :, chunk * width : (chunk + 1) * width] = jnp.dot(
            hidden, w_ref[chunk], preferred_element_type=f32
        ).astype(bf16)
    for pair in range(features // (2 * HEAD)):
        outs = []
        for head in (2 * pair, 2 * pair + 1):
            at = head * HEAD
            queries, key_rows, value_rows = [
                qkv_ref[0, :, part * features + at : part * features + at + HEAD] for part in range(3)
            ]
            weights = soft_scores(queries, key_rows, length).astype(bf16)
            outs.append(jnp.dot(weights, value_rows, preferred_element_type=f32).astype(bf16))
        ctx_ref[0, :, 2 * pair * HEAD : (2 * pair + 2) * HEAD] = jnp.concatenate(outs, axis=1)
    for chunk in range(inner, w_ref.shape[0]):
        at = (chunk - inner) * width
        mid_ref[0, :, at : at + width] = res_ref[0, :, at : at + width] + jnp.dot(
            ctx_ref[0], w_ref[chunk], preferred_element_type=f32
        )
    middle = mid_ref[0]
    normed, _ = norm_rows_of(middle, features)
    hidden = (normed * gain_ref[1:2] + shift_ref[1:2]).astype(bf16)
    hid_ref[0] = hidden
    log_ref[0] = dot_on(hidden, rt_ref[...], 1, 1)


def attention_forward(residual, weight, router_t, gains, shifts, length):
    images, rows, features = residual.shape

    def per_image(width):
        return pl.BlockSpec((1, rows, width), lambda n: (n, 0, 0))

    def whole(shape):
        return pl.BlockSpec(shape, lambda n: (0,) * len(shape), pipeline_mode=pl.Buffered(1))

    extra = router_t.shape[0]
    shape = jax.ShapeDtypeStruct
    return pl.pallas_call(
        functools.partial(attention_kernel, length),
        grid=(images,),
        in_specs=[
            per_image(features), whole(weight.shape), whole(router_t.shape), whole(gains.shape),
            whole(shifts.shape),
        ],
        out_specs=[
            per_image(3 * features), per_image(features), per_image(features), per_image(features),
            per_image(extra),
        ],
        out_shape=[
            shape((images, rows, 3 * features), bf16), shape((images, rows, features), bf16),
            shape((images, rows, features), f32), shape((images, rows, features), bf16),
            shape((images, rows, extra), f32),
        ],
        compiler_params=pltpu.CompilerParams(
            dimension_semantics=("arbitrary",), vmem_limit_bytes=48 * 2**20
        ),
        name="attention_forward",
    )(residual, weight, router_t, gains, shifts)


def norm_back_rows(grad_out, normed, inverse, gain_row, features):
    scaled = grad_out * gain_row
    inner = jnp.sum(scaled, axis=-1, keepdims=True) * (1.0 / features)
    along = jnp.sum(scaled * normed, axis=-1, keepdims=True) * (1.0 / features)
    grad_in = inverse * (scaled - inner - normed * along)
    gain_sum = jnp.sum(grad_out * normed, axis=0, keepdims=True)
    return grad_in, gain_sum, jnp.sum(grad_out, axis=0, keepdims=True)


def attention_back_kernel(
    length, two_ref, grad_ref, res_ref, mid_ref, qkv_ref, ctx_ref, w_ref, gain_ref, shift_ref,
    in_ref, dw_ref, norm_ref, dqkv_ref, sum_ref, norm_sum_ref,
):
    step = pl.program_id(0)
    features = res_ref.shape[2]
    scale = HEAD ** (-0.5)

    @pl.when(step == 0)
    def _():
        sum_ref[...] = jnp.zeros_like(sum_ref)
        norm_sum_ref[...] = jnp.zeros_like(norm_sum_ref)

    normed, inverse = norm_rows_of(mid_ref[0], features)
    grad_in, gain_two, shift_two = norm_back_rows(two_ref[0], normed, inverse, gain_ref[1:2], features)
    grad_middle = grad_ref[0] + grad_in
    in_ref[0] = grad_middle
    grad_attn = grad_middle.astype(bf16)
    width = w_ref.shape[2]
    inner_chunks = 3 * features // width
    grad_context = jnp.zeros(grad_attn.shape, f32)
    for chunk in range(inner_chunks, w_ref.shape[0]):
        at = (chunk - inner_chunks) * width
        part = grad_attn[:, at : at + width]
        sum_ref[chunk] += dot_on(ctx_ref[0], part, 0, 0)
        grad_context += dot_on(part, w_ref[chunk], 1, 1)
    grad_context = grad_context.astype(bf16)
    for pair in range(features // (2 * HEAD)):
        outs = ([], [], [])
        for head in (2 * pair, 2 * pair + 1):
            at = head * HEAD
            queries, key_rows, value_rows = [
                qkv_ref[0, :, part * features + at : part * features + at + HEAD] for part in range(3)
            ]
            grad_head = grad_context[:, at : at + HEAD]
            weights = soft_scores(queries, key_rows, length)
            grad_weights = dot_on(grad_head, value_rows, 1, 1)
            outs[2].append(dot_on(weights.astype(bf16), grad_head, 0, 0))
            inner = jnp.sum(weights * grad_weights, axis=-1, keepdims=True)
            grad_scores = (weights * (grad_weights - inner)).astype(bf16)
            outs[0].append(jnp.dot(grad_scores, key_rows, preferred_element_type=f32) * scale)
            outs[1].append(dot_on(grad_scores, queries, 0, 0) * scale)
        for part in range(3):
            at = part * features + 2 * pair * HEAD
            dqkv_ref[:, at : at + 2 * HEAD] = jnp.concatenate(outs[part], axis=1).astype(bf16)
    normed, inverse = norm_rows_of(res_ref[0], features)
    hidden = (normed * gain_ref[0:1] + shift_ref[0:1]).astype(bf16)
    grad_one = jnp.zeros(normed.shape, f32)
    for chunk in range(inner_chunks):
        part = dqkv_ref[:, chunk * width : (chunk + 1) * width]
        sum_ref[chunk] += dot_on(hidden, part, 0, 0)
        grad_one += dot_on(part, w_ref[chunk], 1, 1)
    grad_in, gain_one, shift_one = norm_back_rows(grad_one, normed, inverse, gain_ref[0:1], features)
    in_ref[0] += grad_in
    for row, value in enumerate((gain_one, gain_two, shift_one, shift_two)):
        norm_sum_ref[row : row + 1] += value

    @pl.when(step == pl.num_programs(0) - 1)
    def _():
        dw_ref[...] = sum_ref[...].astype(bf16)
        norm_ref[...] = norm_sum_ref[...]


def attention_backward(
    grad_two, gradient, residual, middle, qkv_rows, context, weight, gains, shifts, length, wide
):
    images, rows, features = residual.shape

    def per_image(width):
        return pl.BlockSpec((1, rows, width), lambda n: (n, 0, 0))

    def whole(shape):
        return pl.BlockSpec(shape, lambda n: (0,) * len(shape), pipeline_mode=pl.Buffered(1))

    shape = jax.ShapeDtypeStruct
    place = features // weight.shape[2] if wide else 0
    room = weight.shape[:2] + ((place + 1) * weight.shape[2],)
    return pl.pallas_call(
        functools.partial(attention_back_kernel, length),
        grid=(images,),
        in_specs=[per_image(features)] * 4
        + [per_image(3 * features), per_image(features), whole(weight.shape), whole(gains.shape),
           whole(shifts.shape)],
        out_specs=[
            per_image(features),
            pl.BlockSpec(weight.shape, lambda n: (0, 0, place), pipeline_mode=pl.Buffered(1)),
            whole((8, features)),
        ],
        out_shape=[
            shape((images, rows, features), f32), shape(room, bf16),
            shape((8, features), f32),
        ],
        scratch_shapes=[
            pltpu.VMEM((rows, 3 * features), bf16), pltpu.VMEM(weight.shape, f32),
            pltpu.VMEM((8, features), f32),
        ],
        compiler_params=pltpu.CompilerParams(
            dimension_semantics=("arbitrary",), vmem_limit_bytes=56 * 2**20
        ),
        name="attention_backward",
    )(grad_two, gradient, residual, middle, qkv_rows, context, weight, gains, shifts)


def expert_grads(terms, room=None):
    pres, arrived, acts, grads = terms
    groups = len(pres)
    hidden = pres[0].shape[1]
    features = arrived[0].shape[1]
    count = lax.axis_size("replica")
    per = hidden // count
    block = max(per, 384)
    extra = () if room is None else (room,)

    def kernel(*refs):
        out_ref = refs[-1]
        parts = [refs[n * groups : (n + 1) * groups] for n in range(4)]
        for side, (left, right) in enumerate((parts[:2], parts[2:])):
            total = dot_on(left[0][...], right[0][...], 0, 0)
            for n in range(1, groups):
                total += dot_on(left[n][...], right[n][...], 0, 0)
            for n in range(out_ref.shape[0]):
                out_ref[n, side * per : (side + 1) * per] = total[n * per : (n + 1) * per].astype(bf16)

    cut_spec = [pl.BlockSpec((v.shape[0], block), lambda n: (0, n)) for v in pres]
    full_spec = [
        pl.BlockSpec(v.shape, lambda n: (0, 0), pipeline_mode=pl.Buffered(1)) for v in arrived
    ]
    shape = (count, 2 * per, features) if room is None else room.shape
    return pl.pallas_call(
        kernel,
        grid=(hidden // block,),
        in_specs=cut_spec + full_spec + cut_spec + full_spec
        + [pl.BlockSpec(memory_space=pl.ANY)] * len(extra),
        out_specs=pl.BlockSpec((block // per, 2 * per, features), lambda n: (n, 0, 0)),
        out_shape=jax.ShapeDtypeStruct(shape, bf16),
        input_output_aliases={4 * groups: 0} if extra else {},
        compiler_params=pltpu.CompilerParams(
            dimension_semantics=("arbitrary",), vmem_limit_bytes=40 * 2**20
        ),
        name="expert_grads",
    )(*pres, *arrived, *acts, *grads, *extra)


def sum_replica(values):
    return lax.psum_scatter(values, "replica", scatter_dimension=0, tiled=False)


def assemble_experts_kernel(*refs):
    parts, in_ref, out_ref = refs[:-2], refs[-2], refs[-1]
    for layer, part in enumerate(parts):
        per = part.shape[0] // 2
        in_ref[layer, 0] = jnp.transpose(part[:per].astype(f32))
        out_ref[layer, 0] = part[per:].astype(f32)


def assemble_experts(parts):
    rows, features = parts[0].shape
    shape = jax.ShapeDtypeStruct
    return pl.pallas_call(
        assemble_experts_kernel,
        out_shape=[
            shape((len(parts), 1, features, rows // 2), f32),
            shape((len(parts), 1, rows // 2, features), f32),
        ],
        compiler_params=pltpu.CompilerParams(vmem_limit_bytes=40 * 2**20),
        name="assemble_experts",
    )(*parts)


def assemble_kernel(features, starts, rows, part, qkv_ref, out_ref):
    width = part.shape[2]
    inner = 3 * features // width
    for layer, start in enumerate(starts):
        for chunk in range(part.shape[0]):
            values = part[chunk, start : start + rows].astype(f32)
            if chunk < inner:
                qkv_ref[layer, :, chunk * width : (chunk + 1) * width] = values
            else:
                at = (chunk - inner) * width
                out_ref[layer, :, at : at + width] = values


def assemble(tail, features, starts, rows):
    shape = jax.ShapeDtypeStruct
    return pl.pallas_call(
        functools.partial(assemble_kernel, features, starts, rows),
        out_shape=[
            shape((len(starts), rows, 3 * features), f32), shape((len(starts), rows, features), f32)
        ],
        compiler_params=pltpu.CompilerParams(vmem_limit_bytes=40 * 2**20),
        name="assemble",
    )(tail)


def group_list():
    count = lax.axis_size("shard")
    return [list(range(count // 2)), list(range(count // 2, count))]


def expert_forward(arrived, first_weight, second_weight):
    pre_act = jnp.dot(arrived, first_weight, preferred_element_type=f32)
    spread = lax.erf(pre_act * inv_root_two)
    activated = (0.5 * pre_act * (1.0 + spread)).astype(bf16)
    slope = (
        0.5 * (1.0 + spread) + pre_act * jnp.exp(-0.5 * pre_act * pre_act) * inv_root_two_pi
    ).astype(bf16)
    produced = jnp.dot(activated, second_weight, preferred_element_type=f32).astype(bf16)
    return activated, slope, produced


def forward_layer(
    residual, weight, router_t, gains, shifts, first_weight, second_weight, choose, places, length,
    tall,
):
    _, _, features = residual.shape
    experts = len(places)
    qkv_rows, context, middle, hidden_two, logits = attention_forward(
        residual, weight, router_t, gains, shifts, length
    )
    gathered = None
    if tall is not None:
        hidden_two, tall = lax.optimization_barrier((hidden_two, tall))
        gathered = lax.all_gather(tall, "replica", axis=0, tiled=False)
    hidden_two = hidden_two.reshape(-1, features)
    router = jax.nn.softmax(logits.reshape(-1, logits.shape[-1])[:, :experts], axis=-1)
    gates = [jnp.sum(choose[k] * router, axis=1, keepdims=True) for k in range(2)]
    record_moe, picked = [], [0.0, 0.0]
    sent = {}
    for j in sorted(places, reverse=True):
        block = dot_on(places[j][0], hidden_two, 0, 0).astype(bf16)
        sent[j] = swap(block, "shard", j) if j else block
    for group in group_list():
        arrived = jnp.concatenate([sent[j] for j in group], axis=0)
        activated, slope, produced = expert_forward(arrived, first_weight, second_weight)
        capacity = produced.shape[0] // len(group)
        back = {}
        for at, j in reversed(list(enumerate(group))):
            block = produced[at * capacity : (at + 1) * capacity]
            back[j] = swap(block, "shard", j) if j else block
        returned = jnp.concatenate([back[j] for j in group], axis=0)
        for k in range(2):
            single = jnp.concatenate([places[j][1][k] for j in group], axis=1)
            picked[k] = picked[k] + jnp.dot(single, returned, preferred_element_type=f32)
        record_moe.append((arrived, slope, activated))
    mixed = gates[0] * picked[0] + gates[1] * picked[1]
    residual_next = middle + mixed.reshape(middle.shape)
    if gathered is not None:
        residual_next, gathered = lax.optimization_barrier((residual_next, gathered))
    picked = [p.astype(bf16) for p in picked]
    record = (
        residual, qkv_rows, context, middle, hidden_two, router, gates, record_moe, picked,
    )
    return (record, residual_next, gathered)


def backward_layer(
    gradient, record, weight, router_t, gains, shifts, first_weight, second_weight, choose, places,
    length, upper_grad, terms, earlier, last, wide,
):
    residual, qkv_rows, context, middle, hidden_two, router, gates, record_moe, picked = record
    _, _, features = gradient.shape
    experts = len(places)
    flat = gradient.reshape(-1, features)
    scaled = [(gates[k] * flat).astype(bf16) for k in range(2)]
    blocks = {}
    for j in sorted(places, reverse=True):
        singles = places[j][1]
        blocks[j] = (dot_on(singles[0], scaled[0], 0, 0) + dot_on(singles[1], scaled[1], 0, 0)).astype(bf16)
    sent = {}
    for j, block in blocks.items():
        sent[j] = swap(block, "shard", j) if j else block
    grad_two = 0.0
    grad_pres = []
    arriving = []
    summed = None
    if terms is not None:
        terms = after(terms, blocks)
        partial = expert_grads(terms, upper_grad) if wide else (expert_grads(terms), upper_grad)
    for group, (_, slope, _) in zip(group_list(), record_moe):
        grad_arrived = jnp.concatenate([sent[j] for j in group], axis=0)
        if terms is not None and not group[0]:
            grad_arrived, partial, earlier = lax.optimization_barrier((grad_arrived, partial, earlier))
            summed = jax.tree.map(sum_replica, after(partial, earlier))
        grad_act = dot_on(grad_arrived, second_weight, 1, 1)
        grad_pre = (grad_act * slope.astype(f32)).astype(bf16)
        grad_rows = dot_on(grad_pre, first_weight, 1, 1).astype(bf16)
        capacity = grad_rows.shape[0] // len(group)
        back = {}
        for at, j in reversed(list(enumerate(group))):
            block = grad_rows[at * capacity : (at + 1) * capacity]
            back[j] = swap(block, "shard", j) if j else block
        grad_back = jnp.concatenate([back[j] for j in group], axis=0)
        both = jnp.concatenate([places[j][0] for j in group], axis=1)
        grad_two = grad_two + jnp.dot(both, grad_back, preferred_element_type=f32)
        grad_pres.append(grad_pre)
        arriving.append(grad_arrived)
    terms = (grad_pres, [moe[0] for moe in record_moe], [moe[2] for moe in record_moe], arriving)
    own_grads = None
    if last:
        own_grads = expert_grads(terms)
        grad_two, own_grads = lax.optimization_barrier((grad_two, own_grads))
    grad_router = sum(
        choose[k] * jnp.sum(flat * picked[k].astype(f32), axis=1, keepdims=True) for k in range(2)
    )
    grad_logits = (
        router * (grad_router - jnp.sum(router * grad_router, axis=-1, keepdims=True))
    ).astype(bf16)
    grad_router_w = dot_on(grad_logits, hidden_two, 0, 0)
    grad_two = grad_two + jnp.dot(grad_logits, router_t[:experts], preferred_element_type=f32)
    grad_two = grad_two.reshape(gradient.shape)
    input_grad, grad_weight, norm_sums = attention_backward(
        grad_two, gradient, residual, middle, qkv_rows, context, weight, gains, shifts, length,
        wide and not last,
    )
    items = jnp.concatenate([grad_router_w, norm_sums[:4]], axis=0)
    return (input_grad, grad_weight, items, terms, summed, earlier, own_grads)


def shards(
    tokens, expert_ids, qkv_weight, out_weight, router_weight, norm_gain, norm_shift, expert_in,
    expert_out, cotangent,
):
    images, length, features = tokens.shape
    padded = -(-length // 16) * 16
    fill = ((0, 0), (0, padded - length), (0, 0))
    experts = lax.axis_size("shard")
    replicas = lax.axis_size("replica")
    token_count = images * length
    capacity = (8 * token_count + 24 * experts - 1) // (24 * experts) * 8
    packed = jnp.concatenate([qkv_weight, out_weight], axis=2)
    router_all = lax.all_gather(
        jnp.transpose(router_weight, (0, 2, 1)).reshape(LAYERS * experts, -1), "shard", axis=1, tiled=True
    ).reshape(LAYERS, experts, features)
    router_all = jnp.pad(router_all, ((0, 0), (0, -experts % 8), (0, 0)))
    weight = lax.all_gather(gather_shard(packed[0]), "replica", axis=0, tiled=False)
    ids_flat = expert_ids.reshape(-1)
    labels = jnp.arange(experts, dtype=jnp.int32)
    member = (ids_flat[:, None] == labels[None, :]).astype(jnp.int32)
    earlier = jnp.cumsum(member, axis=0) - member
    slot = jnp.sum(earlier * member, axis=1).reshape(expert_ids.shape)
    ids_pair = jnp.pad(expert_ids, fill, constant_values=-1).reshape(-1, 2)
    slot = jnp.pad(slot, fill).reshape(-1, 2)
    choose = [(ids_pair[:, k : k + 1] == labels[None, :]).astype(f32) for k in range(2)]
    slot_row = jnp.arange(capacity, dtype=jnp.int32)[None, :]
    places = {}
    for j in range(experts):
        expert = lax.axis_index("shard") ^ j
        at = jnp.where(ids_pair == expert, slot, -1)
        singles = [(at[:, k : k + 1] == slot_row).astype(bf16) for k in range(2)]
        places[j] = (singles[0] + singles[1], singles)
    residual = jnp.pad(tokens, fill).astype(f32)
    records = []
    weights = []
    for index in range(LAYERS):
        weights.append(weight)
        tall = None
        if index + 1 < LAYERS:
            tall = gather_shard(after(packed[index + 1], weight))
        record, residual, weight = forward_layer(
            residual, weight, router_all[index], norm_gain[index], norm_shift[index],
            expert_in[index, 0], expert_out[index, 0], choose, places, length, tall,
        )
        records.append(record)
    activations = residual[:, :length].astype(bf16)
    gradient = jnp.pad(cotangent, fill).astype(f32)
    items = [None] * LAYERS
    grad_weight, terms, summed = None, None, ()
    wide = 2 * (expert_in.shape[3] // replicas) == features and features % (4 * features // replicas) == 0
    for index in range(LAYERS - 1, -1, -1):
        gradient, grad_weight, items[index], terms, summed, earlier, own_grads = backward_layer(
            gradient, records[index], weights[index], router_all[index], norm_gain[index],
            norm_shift[index], expert_in[index, 0], expert_out[index, 0], choose, places, length,
            grad_weight, terms, () if summed is None else summed, index == 0, wide,
        )
    input_grad = gradient[:, :length]
    rows = features // experts
    width = grad_weight.shape[-1]
    count = items[0].shape[0]
    small = jnp.stack(items, axis=1).astype(bf16).reshape(count, LAYERS, experts, rows)
    small = jnp.pad(
        jnp.transpose(small, (0, 2, 1, 3)), ((0, replicas - count), (0, 0), (0, 8 - LAYERS), (0, width - rows))
    )
    chunks = jnp.concatenate([grad_weight.reshape(replicas, experts, rows, width), small], axis=2)
    whole, (summed, earlier) = scatter_replica(chunks[None], summed, earlier)
    whole = whole[0]
    upper = [split_sum(part, features) for part in (summed, earlier)]
    upper_dense = jnp.concatenate([part[1] for part in upper], axis=1)
    upper_dense = upper_dense.reshape(experts, -1, upper_dense.shape[1])
    for bit in bits_from("shard", 1)[::-1]:
        upper_dense = add_swapped(upper_dense, "shard", bit, bit, 0)
    upper_dense = upper_dense[0]
    own_sum = sum_replica(after(own_grads, summed))
    for bit in bits_from("shard", 1)[::-1]:
        whole = add_swapped(whole, "shard", bit, bit, 0)
    whole = jnp.concatenate(
        [whole[0]] + [upper_dense[:, n * width : (n + 1) * width] for n in range(LAYERS - 1)], axis=0
    )[None]
    expert_in_grad, expert_out_grad = assemble_experts([own_sum] + [part[0] for part in upper])
    whole, expert_in_grad, expert_out_grad = lax.optimization_barrier(
        (whole, expert_in_grad, expert_out_grad)
    )
    tail = gather_replica(whole)[0]
    small = tail[:count, rows : rows + LAYERS, :rows].astype(f32)
    qkv_grad, out_grad = assemble(tail, features, [0, rows + 8, 2 * rows + 8], rows)
    router_grad = jnp.transpose(small[:experts], (1, 2, 0))
    norm_grads = jnp.transpose(small[experts:], (1, 0, 2))
    gain_grad = norm_grads[:, :2]
    shift_grad = norm_grads[:, 2:]
    return (
        activations, input_grad, qkv_grad, out_grad, router_grad, gain_grad, shift_grad,
        expert_in_grad, expert_out_grad,
    )


def solution(mesh):
    in_specs = (
        P(("replica", "shard"), None, None),
        P(("replica", "shard"), None, None),
        P(None, "shard", None),
        P(None, "shard", None),
        P(None, "shard", None),
        P(),
        P(),
        P(None, "shard", None, None),
        P(None, "shard", None, None),
        P(("replica", "shard"), None, None),
    )
    out_specs = (
        P(("replica", "shard"), None, None),
        P(("replica", "shard"), None, None),
        P(None, "shard", None),
        P(None, "shard", None),
        P(None, "shard", None),
        P(None, None, "shard"),
        P(None, None, "shard"),
        P(None, "shard", None, "replica"),
        P(None, "shard", "replica", None),
    )
    return jax.shard_map(shards, mesh=mesh, in_specs=in_specs, out_specs=out_specs, check_vma=False)
```

profile of v0, /device:TPU:0, one launch (start us, length us, event | category | flops | bytes accessed | tf_op | source)
XLA Modules:
  0.0 1001.7 jit_solution(11521399036257269467)
XLA Ops:
  10.9 22.1 %all_to_all.15 = bf16[4,192,384]{2,1,0:T(8,128)(2,1)} all-to-all(bf16[4,192,384]{2,1,0:T(8,128)(2,1)S(1)} %broadcast_in_dim.22), channel_id=1, replica_groups=mesh['replica'=8,'shard'=4] {'shard'}, dimensions={0} | all-to-all | bytes 1179648 | tf_op jit(solution)/shard_map/all_to_all | solution.py:116
  33.4 13.1 %all-gather.2 = bf16[4,192,12]{1,2,0:T(8,128)(2,1)S(1)} all-gather(bf16[1,192,12]{1,2,0:T(8,128)(2,1)S(1)} %bitcast.428), channel_id=1, replica_groups=mesh['replica'=8,'shard'=4] {'shard'}, dimensions={0}, use_global_device_ids=true | all-gather | bytes 23040 | tf_op jit(solution)/shard_map/all_gather | solution.py:548
  50.8 20.3 %all-gather.7.cloned.1.call-done.w_ref = bf16[8,768,384]{2,1,0:T(8,128)(2,1)} async-done(((bf16[1,768,384]{2,1,0:T(8,128)(2,1)}), bf16[8,768,384]{2,1,0:T(8,128)(2,1)}) %all-gather.7.cloned.1.call-update) | async-done | bytes 4718608 | tf_op jit(solution)/shard_map/all_gather | solution.py:552
  72.0 4.6 all-to-all-start.1
  80.2 11.0 %attention_forward.3 = (bf16[2,208,2304]{2,1,0:T(8,128)(2,1)S(1)}, bf16[2,208,768]{2,1,0:T(8,128)(2,1)S(1)}, f32[2,208,768]{2,1,0:T(8,128)S(1)}, bf16[2,208,768]{2,1,0:T(8,128)(2,1)S(1)}, f32[2,208,8]{2,1,0:T(8,128)S(1)}) custom-call(f32[2,208,768]{2,1,0:T(8,128)S(1)} %pad_convert_fusion.1.res_ref, bf16[8,768,384]{2,1,0:T(8,128)(2,1)} %all-gather.7.cloned.1.call-done.w_ref, ...), custom_call_target="tpu_custom_call" | custom-call | tf_op jit(solution)/shard_map/attention_forward/pallas_call | solution.py:186
  108.9 21.9 %collective-permute-done.2 = bf16[264,768]{1,0:T(8,128)(2,1)S(1)} collective-permute-done((bf16[264,768]{1,0:T(8,128)(2,1)S(1)}, bf16[264,768]{1,0:T(8,128)(2,1)S(1)}, u32[]{:S(2)}, u32[]{:S(2)}) %collective-permute-start.2) | collective-permute-done | bytes 405536 | tf_op jit(solution)/shard_map/ppermute | solution.py:29
  130.9 6.8 multiply_convert_fusion.10
  144.9 7.5 collective-permute-start.4
  152.4 15.3 %multiply_convert_fusion.11 = (bf16[528,3072]{1,0:T(8,128)(2,1)S(1)}, f32[528,3072]{1,0:T(8,128)}) fusion(bf16[3,1,768,3072]{3,2,1,0:T(8,128)(2,1)} %param.17, bf16[264,768]{1,0:T(8,128)(2,1)S(1)} %collective-permute-done, bf16[264,768]{1,0:T(8,128)(2,1)S(1)} %convolution_convert_fusion.11), kind=kOutput, calls=%fused_computation.54 | convolution fusion | flops 2501148672 | bytes 15261696 | tf_op jit(solution)/shard_map/dot_general | solution.py:418
  171.0 9.3 collective-permute-done.4
  181.8 7.1 collective-permute-done.1
  193.6 4.8 all-to-all-start.2
  198.4 11.0 %attention_forward.4 = (bf16[2,208,2304]{2,1,0:T(8,128)(2,1)S(1)}, bf16[2,208,768]{2,1,0:T(8,128)(2,1)S(1)}, f32[2,208,768]{2,1,0:T(8,128)S(1)}, bf16[2,208,768]{2,1,0:T(8,128)(2,1)S(1)}, f32[2,208,8]{2,1,0:T(8,128)S(1)}) custom-call(f32[2,208,768]{2,1,0:T(8,128)S(1)} %add.265.res_ref, bf16[8,768,384]{2,1,0:T(8,128)(2,1)} %bitcast.358, ...), custom_call_target="tpu_custom_call" | custom-call | tf_op jit(solution)/shard_map/attention_forward/pallas_call | solution.py:186
  211.5 3.0 all-to-all-done.2
  233.7 20.3 %collective-permute-done.8 = bf16[264,768]{1,0:T(8,128)(2,1)S(1)} collective-permute-done((bf16[264,768]{1,0:T(8,128)(2,1)S(1)}, bf16[264,768]{1,0:T(8,128)(2,1)S(1)}, u32[]{:S(2)}, u32[]{:S(2)}) %collective-permute-start.8) | collective-permute-done | bytes 405536 | tf_op jit(solution)/shard_map/ppermute | solution.py:29
  254.1 7.0 multiply_convert_fusion.8
  266.9 8.2 collective-permute-start.10
  275.1 6.6 multiply_convert_fusion.9
  284.7 19.0 %collective-permute-done.10 = bf16[264,768]{1,0:T(8,128)(2,1)S(1)} collective-permute-done((bf16[264,768]{1,0:T(8,128)(2,1)S(1)}, bf16[264,768]{1,0:T(8,128)(2,1)S(1)}, u32[]{:S(2)}, u32[]{:S(2)}) %collective-permute-start.10) | collective-permute-done | bytes 405536 | tf_op jit(solution)/shard_map/ppermute | solution.py:29
  307.9 11.4 %attention_forward.5 = (bf16[2,208,2304]{2,1,0:T(8,128)(2,1)S(1)}, bf16[2,208,768]{2,1,0:T(8,128)(2,1)S(1)}, f32[2,208,768]{2,1,0:T(8,128)S(1)}, bf16[2,208,768]{2,1,0:T(8,128)(2,1)S(1)}, f32[2,208,8]{2,1,0:T(8,128)S(1)}) custom-call(f32[2,208,768]{2,1,0:T(8,128)S(1)} %add.271.res_ref, bf16[8,768,384]{2,1,0:T(8,128)(2,1)} %bitcast.360, ...), custom_call_target="tpu_custom_call" | custom-call | tf_op jit(solution)/shard_map/attention_forward/pallas_call | solution.py:186
  329.0 23.8 %collective-permute-done.14 = bf16[264,768]{1,0:T(8,128)(2,1)S(1)} collective-permute-done((bf16[264,768]{1,0:T(8,128)(2,1)S(1)}, bf16[264,768]{1,0:T(8,128)(2,1)S(1)}, u32[]{:S(2)}, u32[]{:S(2)}) %collective-permute-start.14) | collective-permute-done | bytes 405536 | tf_op jit(solution)/shard_map/ppermute | solution.py:29
  352.9 6.7 multiply_convert_fusion.6
  364.0 9.2 collective-permute-start.16
  373.2 6.7 multiply_convert_fusion.7
  385.3 15.6 %collective-permute-done.16 = bf16[264,768]{1,0:T(8,128)(2,1)S(1)} collective-permute-done((bf16[264,768]{1,0:T(8,128)(2,1)S(1)}, bf16[264,768]{1,0:T(8,128)(2,1)S(1)}, u32[]{:S(2)}, u32[]{:S(2)}) %collective-permute-start.16) | collective-permute-done | bytes 405536 | tf_op jit(solution)/shard_map/ppermute | solution.py:29
  402.4 6.4 collective-permute-done.13
  426.8 29.6 %collective-permute-done.20 = bf16[264,768]{1,0:T(8,128)(2,1)S(1)} collective-permute-done((bf16[264,768]{1,0:T(8,128)(2,1)S(1)}, bf16[264,768]{1,0:T(8,128)(2,1)S(1)}, u32[]{:S(2)}, u32[]{:S(2)}) %collective-permute-start.20) | collective-permute-done | bytes 405536 | tf_op jit(solution)/shard_map/ppermute | solution.py:29
  456.5 6.7 multiply_convert_fusion.4.refs_1_
  463.2 5.1 fusion.136
  470.8 6.2 multiply_convert_fusion.5.refs_0_
  477.0 6.2 fusion.133
  485.2 11.8 %collective-permute-done.22 = bf16[264,768]{1,0:T(8,128)(2,1)S(1)} collective-permute-done((bf16[264,768]{1,0:T(8,128)(2,1)S(1)}, bf16[264,768]{1,0:T(8,128)(2,1)S(1)}, u32[]{:S(2)}, u32[]{:S(2)}) %collective-permute-start.22) | collective-permute-done | bytes 405536 | tf_op jit(solution)/shard_map/ppermute | solution.py:29
  497.7 7.8 collective-permute-done.19
  507.4 28.7 %attention_backward.3 = (f32[2,208,768]{2,1,0:T(8,128)}, bf16[8,768,1152]{2,1,0:T(8,128)(2,1)}, f32[8,768]{1,0:T(8,128)}) custom-call(f32[2,208,768]{2,1,0:T(8,128)} %bitcast.371, f32[2,208,768]{2,1,0:T(8,128)} %pad_convert_fusion.grad_ref, f32[2,208,768]{2,1,0:T(8,128)} %copy-done.2, f32[2,208,768]{2,1,0:T(8,128)} %copy-done.5, ...), custom_call_target="tpu_custom_call" | custom-call | tf_op jit(solution)/shard_map/attention_backward/pallas_call | solution.py:295
  551.3 19.2 %expert_grads.3 = bf16[8,768,1152]{2,1,0:T(8,128)(2,1)} custom-call(bf16[528,3072]{1,0:T(8,128)(2,1)S(1)} %copy-done.14, bf16[528,3072]{1,0:T(8,128)(2,1)S(1)} %multiply_convert_fusion.4.refs_1_, bf16[528,768]{1,0:T(8,128)(2,1)S(1)} %pad_maximum_fusion.9.refs_2_, bf16[528,768]{1,0:T(8,128)(2,1)S(1)} %copy-done.23, ...), custom_call_target="tpu_custom_call", output_to_operand_aliasing={{}: (8, {})} | custom-call | tf_op jit(solution)/shard_map/expert_grads/pallas_call | solution.py:346
  578.5 23.1 %collective-permute-done.26 = bf16[264,768]{1,0:T(8,128)(2,1)S(1)} collective-permute-done((bf16[264,768]{1,0:T(8,128)(2,1)}, bf16[264,768]{1,0:T(8,128)(2,1)S(1)}, u32[]{:S(2)}, u32[]{:S(2)}) %collective-permute-start.26) | collective-permute-done | bytes 405536 | tf_op jit(solution)/shard_map/ppermute | solution.py:29
  601.8 7.6 multiply_convert_fusion.2.refs_1_
  612.2 9.2 collective-permute-start.28
  624.0 6.3 multiply_convert_fusion.3.refs_0_
  633.8 15.4 %collective-permute-done.28 = bf16[264,768]{1,0:T(8,128)(2,1)S(1)} collective-permute-done((bf16[264,768]{1,0:T(8,128)(2,1)S(1)}, bf16[264,768]{1,0:T(8,128)(2,1)S(1)}, u32[]{:S(2)}, u32[]{:S(2)}) %collective-permute-start.28) | collective-permute-done | bytes 405536 | tf_op jit(solution)/shard_map/ppermute | solution.py:29
  649.8 7.4 collective-permute-done.25
  659.0 28.8 %attention_backward.4 = (f32[2,208,768]{2,1,0:T(8,128)}, bf16[8,768,1152]{2,1,0:T(8,128)(2,1)}, f32[8,768]{1,0:T(8,128)}) custom-call(f32[2,208,768]{2,1,0:T(8,128)} %bitcast.370, f32[2,208,768]{2,1,0:T(8,128)} %get-tuple-element.99.grad_ref, f32[2,208,768]{2,1,0:T(8,128)} %copy-done.1, f32[2,208,768]{2,1,0:T(8,128)} %copy-done.4, ...), custom_call_target="tpu_custom_call" | custom-call | tf_op jit(solution)/shard_map/attention_backward/pallas_call | solution.py:295
  701.7 19.3 %expert_grads.4 = bf16[8,768,1152]{2,1,0:T(8,128)(2,1)} custom-call(bf16[528,3072]{1,0:T(8,128)(2,1)S(1)} %copy-done.12, bf16[528,3072]{1,0:T(8,128)(2,1)S(1)} %multiply_convert_fusion.2.refs_1_, bf16[528,768]{1,0:T(8,128)(2,1)S(1)} %pad_maximum_fusion.7.refs_2_, bf16[528,768]{1,0:T(8,128)(2,1)S(1)} %copy-done.21, ...), custom_call_target="tpu_custom_call", output_to_operand_aliasing={{}: (8, {})} | custom-call | tf_op jit(solution)/shard_map/expert_grads/pallas_call | solution.py:346
  729.2 3.4 multiply_reduce_fusion.1
  737.5 27.0 %collective-permute-done.32 = bf16[264,768]{1,0:T(8,128)(2,1)S(1)} collective-permute-done((bf16[264,768]{1,0:T(8,128)(2,1)}, bf16[264,768]{1,0:T(8,128)(2,1)S(1)}, u32[]{:S(2)}, u32[]{:S(2)}) %collective-permute-start.32) | collective-permute-done | bytes 405536 | tf_op jit(solution)/shard_map/ppermute | solution.py:29
  764.6 7.3 multiply_convert_fusion.refs_1_
  771.9 5.0 fusion.112
  779.4 6.8 multiply_convert_fusion.1.refs_0_
  786.3 5.1 fusion.109
  794.2 11.2 %collective-permute-done.34 = bf16[264,768]{1,0:T(8,128)(2,1)S(1)} collective-permute-done((bf16[264,768]{1,0:T(8,128)(2,1)S(1)}, bf16[264,768]{1,0:T(8,128)(2,1)S(1)}, u32[]{:S(2)}, u32[]{:S(2)}) %collective-permute-start.34) | collective-permute-done | bytes 405536 | tf_op jit(solution)/shard_map/ppermute | solution.py:29
  807.2 19.3 %expert_grads.5 = bf16[8,768,768]{2,1,0:T(8,128)(2,1)} custom-call(bf16[528,3072]{1,0:T(8,128)(2,1)S(1)} %multiply_convert_fusion.1.refs_0_, bf16[528,3072]{1,0:T(8,128)(2,1)S(1)} %multiply_convert_fusion.refs_1_, bf16[528,768]{1,0:T(8,128)(2,1)S(1)} %pad_maximum_fusion.5.refs_2_, bf16[528,768]{1,0:T(8,128)(2,1)S(1)} %copy-done.19, ...), custom_call_target="tpu_custom_call" | custom-call | tf_op jit(solution)/shard_map/expert_grads/pallas_call | solution.py:346
  830.0 28.5 %attention_backward.5 = (f32[2,208,768]{2,1,0:T(8,128)}, bf16[8,768,384]{2,1,0:T(8,128)(2,1)}, f32[8,768]{1,0:T(8,128)}) custom-call(f32[2,208,768]{2,1,0:T(8,128)} %bitcast.374, f32[2,208,768]{2,1,0:T(8,128)} %get-tuple-element.112.grad_ref, f32[2,208,768]{2,1,0:T(8,128)} %copy-done, f32[2,208,768]{2,1,0:T(8,128)} %copy-done.3, ...), custom_call_target="tpu_custom_call" | custom-call | tf_op jit(solution)/shard_map/attention_backward/pallas_call | solution.py:295
  861.5 4.8 collective-permute-done.36
  866.3 3.0 fusion.30
  877.2 9.4 collective-permute-start.43
  891.7 21.3 %collective-permute-done.43 = bf16[2,192,768]{2,1,0:T(8,128)(2,1)} collective-permute-done((bf16[2,192,768]{2,1,0:T(8,128)(2,1)}, bf16[2,192,768]{2,1,0:T(8,128)(2,1)}, u32[]{:S(2)}, u32[]{:S(2)}) %collective-permute-start.43) | collective-permute-done | bytes 589856 | tf_op jit(solution)/shard_map/ppermute | solution.py:29
  917.8 14.8 %collective-permute-done.40 = bf16[1,1,4,104,384]{4,3,2,1,0:T(8,128)(2,1)S(1)} collective-permute-done((bf16[1,1,4,104,384]{4,3,2,1,0:T(8,128)(2,1)S(1)}, bf16[1,1,4,104,384]{4,3,2,1,0:T(8,128)(2,1)S(1)}, u32[]{:S(2)}, u32[]{:S(2)}) %collective-permute-start.40) | collective-permute-done | bytes 319520 | tf_op jit(solution)/shard_map/ppermute | solution.py:29
  936.7 10.8 %collective-permute-done.41 = bf16[2,200,384]{2,1,0:T(8,128)(2,1)} collective-permute-done((bf16[2,200,384]{2,1,0:T(8,128)(2,1)S(1)}, bf16[2,200,384]{2,1,0:T(8,128)(2,1)}, u32[]{:S(2)}, u32[]{:S(2)}) %collective-permute-start.41) | collective-permute-done | bytes 307232 | tf_op jit(solution)/shard_map/ppermute | solution.py:29
  948.7 5.8 collective-permute-done.42
  954.6 4.6 reduce-scatter.8.cloned.1.call-done
  960.5 3.5 assemble_experts.1
  966.3 4.9 collective-permute-done.45
  973.5 8.7 collective-permute-done.46
  989.2 3.4 assemble.1
  (627 shorter events, 238.2 us)
Async XLA Ops:
  7.2 63.9 %all-gather.7.cloned.1.call-start = ((), (), s32[]{:S(2)}) async-start(), calls=%async_computation.6 | async-start | bytes 5308416 | tf_op jit(solution)/shard_map/all_gather | solution.py:552
  72.0 21.3 %all-to-all-start.1 = ((bf16[4,192,384]{2,1,0:T(8,128)(2,1)}), bf16[4,192,384]{2,1,0:T(8,128)(2,1)}, u32[]{:S(2)}, u32[]{:S(2)}) async-start(bf16[4,192,384]{2,1,0:T(8,128)(2,1)} %broadcast_in_dim.24), calls=%async_computation.1 | async-start | bytes 1179648 | tf_op jit(solution)/shard_map/all_to_all | solution.py:116
  76.6 115.0 %all-gather.9.cloned.1.call-start = ((), (), s32[]{:S(2)}) async-start(), calls=%async_computation.10 | async-start | bytes 5308416 | tf_op jit(solution)/shard_map/all_gather | solution.py:440
  77.2 121.2 %copy-start.38 = (f32[2,768]{1,0:T(2,128)}, f32[2,768]{1,0:T(2,128)S(1)}, u32[]{:S(2)}) copy-start(f32[2,768]{1,0:T(2,128)S(1)} %get-tuple-element.248.shift_ref) | copy-start | bytes 18436
  77.2 121.2 %copy-start.39 = (f32[2,768]{1,0:T(2,128)}, f32[2,768]{1,0:T(2,128)S(1)}, u32[]{:S(2)}) copy-start(f32[2,768]{1,0:T(2,128)S(1)} %get-tuple-element.289.gain_ref) | copy-start | bytes 18436
  77.2 230.7 %copy-start.40 = (f32[2,768]{1,0:T(2,128)}, f32[2,768]{1,0:T(2,128)S(1)}, u32[]{:S(2)}) copy-start(f32[2,768]{1,0:T(2,128)S(1)} %get-tuple-element.246.shift_ref) | copy-start | bytes 18436
  77.2 230.7 %copy-start.41 = (f32[2,768]{1,0:T(2,128)}, f32[2,768]{1,0:T(2,128)S(1)}, u32[]{:S(2)}) copy-start(f32[2,768]{1,0:T(2,128)S(1)} %get-tuple-element.291.gain_ref) | copy-start | bytes 18436
  93.3 98.1 %copy-start.3 = (f32[2,208,768]{2,1,0:T(8,128)}, f32[2,208,768]{2,1,0:T(8,128)S(1)}, u32[]{:S(2)}) copy-start(f32[2,208,768]{2,1,0:T(8,128)S(1)} %get-tuple-element.78.mid_ref) | copy-start | bytes 3833860
  100.1 30.7 %collective-permute-start.2 = (bf16[264,768]{1,0:T(8,128)(2,1)S(1)}, bf16[264,768]{1,0:T(8,128)(2,1)S(1)}, u32[]{:S(2)}, u32[]{:S(2)}) collective-permute-start(bf16[264,768]{1,0:T(8,128)(2,1)S(1)} %convolution_convert_fusion.9), channel_id=1, source_target_pairs={{0,2},{1,3},{2,0},{3,1},{4,6},{5,7},{6,4},{7,5},{8,10},{9,11},{10,... | collective-permute-start | bytes 1216520 | tf_op jit(solution)/shard_map/ppermute | solution.py:29
  104.4 26.4 %collective-permute-start.3 = (bf16[264,768]{1,0:T(8,128)(2,1)S(1)}, bf16[264,768]{1,0:T(8,128)(2,1)S(1)}, u32[]{:S(2)}, u32[]{:S(2)}) collective-permute-start(bf16[264,768]{1,0:T(8,128)(2,1)S(1)} %convolution_convert_fusion.8), channel_id=1, source_target_pairs={{0,3},{1,2},{2,1},{3,0},{4,7},{5,6},{6,5},{7,4},{8,11},{9,10},{10,... | collective-permute-start | bytes 1216520 | tf_op jit(solution)/shard_map/ppermute | solution.py:29
  107.3 45.1 %collective-permute-start = (bf16[264,768]{1,0:T(8,128)(2,1)S(1)}, bf16[264,768]{1,0:T(8,128)(2,1)S(1)}, u32[]{:S(2)}, u32[]{:S(2)}) collective-permute-start(bf16[264,768]{1,0:T(8,128)(2,1)S(1)} %convolution_convert_fusion.10), channel_id=1, source_target_pairs={{0,1},{1,0},{2,3},{3,2},{4,5},{5,4},{6,7},{7,6},{8,9},{9,8},{10,11... | collective-permute-start | bytes 1216520 | tf_op jit(solution)/shard_map/ppermute | solution.py:29
  142.0 38.4 %collective-permute-start.5 = (bf16[264,768]{1,0:T(8,128)(2,1)S(1)}, bf16[264,768]{1,0:T(8,128)(2,1)S(1)}, u32[]{:S(2)}, u32[]{:S(2)}) collective-permute-start(bf16[264,768]{1,0:T(8,128)(2,1)S(1)} %get-tuple-element.236), channel_id=1, source_target_pairs={{0,3},{1,2},{2,1},{3,0},{4,7},{5,6},{6,5},{7,4},{8,11},{9,10},{10,... | collective-permute-start | bytes 1216520 | tf_op jit(solution)/shard_map/ppermute | solution.py:29
  144.9 35.5 %collective-permute-start.4 = (bf16[264,768]{1,0:T(8,128)(2,1)S(1)}, bf16[264,768]{1,0:T(8,128)(2,1)S(1)}, u32[]{:S(2)}, u32[]{:S(2)}) collective-permute-start(bf16[264,768]{1,0:T(8,128)(2,1)S(1)} %get-tuple-element.237), channel_id=1, source_target_pairs={{0,2},{1,3},{2,0},{3,1},{4,6},{5,7},{6,4},{7,5},{8,10},{9,11},{10,... | collective-permute-start | bytes 1216520 | tf_op jit(solution)/shard_map/ppermute | solution.py:29
  170.5 18.4 %collective-permute-start.1 = (bf16[264,768]{1,0:T(8,128)(2,1)S(1)}, bf16[264,768]{1,0:T(8,128)(2,1)S(1)}, u32[]{:S(2)}, u32[]{:S(2)}) collective-permute-start(bf16[264,768]{1,0:T(8,128)(2,1)S(1)} %get-tuple-element.235), channel_id=1, source_target_pairs={{0,1},{1,0},{2,3},{3,2},{4,5},{5,4},{6,7},{7,6},{8,9},{9,8},{10,11... | collective-permute-start | bytes 1216520 | tf_op jit(solution)/shard_map/ppermute | solution.py:29
  193.6 21.0 %all-to-all-start.2 = ((bf16[4,192,384]{2,1,0:T(8,128)(2,1)}), bf16[4,192,384]{2,1,0:T(8,128)(2,1)}, u32[]{:S(2)}, u32[]{:S(2)}) async-start(bf16[4,192,384]{2,1,0:T(8,128)(2,1)} %broadcast_in_dim.25), calls=%async_computation.2 | async-start | bytes 1179648 | tf_op jit(solution)/shard_map/all_to_all | solution.py:116
  198.4 109.5 %all-gather.11.cloned.1.call-start = ((), (), s32[]{:S(2)}) async-start(), calls=%async_computation.11 | async-start | bytes 5308416 | tf_op jit(solution)/shard_map/all_gather | solution.py:440
  211.5 96.1 %copy-start.4 = (f32[2,208,768]{2,1,0:T(8,128)}, f32[2,208,768]{2,1,0:T(8,128)S(1)}, u32[]{:S(2)}) copy-start(f32[2,208,768]{2,1,0:T(8,128)S(1)} %get-tuple-element.86.mid_ref) | copy-start | bytes 3833860
  214.6 506.5 %reduce-scatter.4.cloned.1.call-start = ((), (), s32[]{:S(2)}) async-start(), calls=%async_computation.7 | async-start | bytes 15925248 | tf_op jit(solution)/shard_map/reduce_scatter | solution.py:362
  225.9 28.1 %collective-permute-start.8 = (bf16[264,768]{1,0:T(8,128)(2,1)S(1)}, bf16[264,768]{1,0:T(8,128)(2,1)S(1)}, u32[]{:S(2)}, u32[]{:S(2)}) collective-permute-start(bf16[264,768]{1,0:T(8,128)(2,1)S(1)} %convolution_convert_fusion.5), channel_id=1, source_target_pairs={{0,2},{1,3},{2,0},{3,1},{4,6},{5,7},{6,4},{7,5},{8,10},{9,11},{10,... | collective-permute-start | bytes 1216520 | tf_op jit(solution)/shard_map/ppermute | solution.py:29
  227.6 26.4 %collective-permute-start.9 = (bf16[264,768]{1,0:T(8,128)(2,1)S(1)}, bf16[264,768]{1,0:T(8,128)(2,1)S(1)}, u32[]{:S(2)}, u32[]{:S(2)}) collective-permute-start(bf16[264,768]{1,0:T(8,128)(2,1)S(1)} %convolution_convert_fusion.4), channel_id=1, source_target_pairs={{0,3},{1,2},{2,1},{3,0},{4,7},{5,6},{6,5},{7,4},{8,11},{9,10},{10,... | collective-permute-start | bytes 1216520 | tf_op jit(solution)/shard_map/ppermute | solution.py:29
  230.5 44.6 %collective-permute-start.6 = (bf16[264,768]{1,0:T(8,128)(2,1)S(1)}, bf16[264,768]{1,0:T(8,128)(2,1)S(1)}, u32[]{:S(2)}, u32[]{:S(2)}) collective-permute-start(bf16[264,768]{1,0:T(8,128)(2,1)S(1)} %convolution_convert_fusion.6), channel_id=1, source_target_pairs={{0,1},{1,0},{2,3},{3,2},{4,5},{5,4},{6,7},{7,6},{8,9},{9,8},{10,11... | collective-permute-start | bytes 1216520 | tf_op jit(solution)/shard_map/ppermute | solution.py:29
  264.5 39.3 %collective-permute-start.11 = (bf16[264,768]{1,0:T(8,128)(2,1)S(1)}, bf16[264,768]{1,0:T(8,128)(2,1)S(1)}, u32[]{:S(2)}, u32[]{:S(2)}) collective-permute-start(bf16[264,768]{1,0:T(8,128)(2,1)S(1)} %get-tuple-element.232), channel_id=1, source_target_pairs={{0,3},{1,2},{2,1},{3,0},{4,7},{5,6},{6,5},{7,4},{8,11},{9,10},{10,... | collective-permute-start | bytes 1216520 | tf_op jit(solution)/shard_map/ppermute | solution.py:29
  266.9 36.8 %collective-permute-start.10 = (bf16[264,768]{1,0:T(8,128)(2,1)S(1)}, bf16[264,768]{1,0:T(8,128)(2,1)S(1)}, u32[]{:S(2)}, u32[]{:S(2)}) collective-permute-start(bf16[264,768]{1,0:T(8,128)(2,1)S(1)} %get-tuple-element.233), channel_id=1, source_target_pairs={{0,2},{1,3},{2,0},{3,1},{4,6},{5,7},{6,4},{7,5},{8,10},{9,11},{10,... | collective-permute-start | bytes 1216520 | tf_op jit(solution)/shard_map/ppermute | solution.py:29
  284.6 20.7 %collective-permute-start.7 = (bf16[264,768]{1,0:T(8,128)(2,1)S(1)}, bf16[264,768]{1,0:T(8,128)(2,1)S(1)}, u32[]{:S(2)}, u32[]{:S(2)}) collective-permute-start(bf16[264,768]{1,0:T(8,128)(2,1)S(1)} %get-tuple-element.231), channel_id=1, source_target_pairs={{0,1},{1,0},{2,3},{3,2},{4,5},{5,4},{6,7},{7,6},{8,9},{9,8},{10,11... | collective-permute-start | bytes 1216520 | tf_op jit(solution)/shard_map/ppermute | solution.py:29
  323.3 29.4 %collective-permute-start.14 = (bf16[264,768]{1,0:T(8,128)(2,1)S(1)}, bf16[264,768]{1,0:T(8,128)(2,1)S(1)}, u32[]{:S(2)}, u32[]{:S(2)}) collective-permute-start(bf16[264,768]{1,0:T(8,128)(2,1)S(1)} %convolution_convert_fusion.1), channel_id=1, source_target_pairs={{0,2},{1,3},{2,0},{3,1},{4,6},{5,7},{6,4},{7,5},{8,10},{9,11},{10,... | collective-permute-start | bytes 1216520 | tf_op jit(solution)/shard_map/ppermute | solution.py:29
  323.6 29.3 %collective-permute-start.15 = (bf16[264,768]{1,0:T(8,128)(2,1)S(1)}, bf16[264,768]{1,0:T(8,128)(2,1)S(1)}, u32[]{:S(2)}, u32[]{:S(2)}) collective-permute-start(bf16[264,768]{1,0:T(8,128)(2,1)S(1)} %convolution_convert_fusion), channel_id=1, source_target_pairs={{0,3},{1,2},{2,1},{3,0},{4,7},{5,6},{6,5},{7,4},{8,11},{9,10},{10,... | collective-permute-start | bytes 1216520 | tf_op jit(solution)/shard_map/ppermute | solution.py:29
  326.2 47.0 %collective-permute-start.12 = (bf16[264,768]{1,0:T(8,128)(2,1)S(1)}, bf16[264,768]{1,0:T(8,128)(2,1)S(1)}, u32[]{:S(2)}, u32[]{:S(2)}) collective-permute-start(bf16[264,768]{1,0:T(8,128)(2,1)S(1)} %convolution_convert_fusion.2), channel_id=1, source_target_pairs={{0,1},{1,0},{2,3},{3,2},{4,5},{5,4},{6,7},{7,6},{8,9},{9,8},{10,11... | collective-permute-start | bytes 1216520 | tf_op jit(solution)/shard_map/ppermute | solution.py:29
  364.0 36.9 %collective-permute-start.16 = (bf16[264,768]{1,0:T(8,128)(2,1)S(1)}, bf16[264,768]{1,0:T(8,128)(2,1)S(1)}, u32[]{:S(2)}, u32[]{:S(2)}) collective-permute-start(bf16[264,768]{1,0:T(8,128)(2,1)S(1)} %get-tuple-element.229), channel_id=1, source_target_pairs={{0,2},{1,3},{2,0},{3,1},{4,6},{5,7},{6,4},{7,5},{8,10},{9,11},{10,... | collective-permute-start | bytes 1216520 | tf_op jit(solution)/shard_map/ppermute | solution.py:29
  382.6 18.3 %collective-permute-start.17 = (bf16[264,768]{1,0:T(8,128)(2,1)S(1)}, bf16[264,768]{1,0:T(8,128)(2,1)S(1)}, u32[]{:S(2)}, u32[]{:S(2)}) collective-permute-start(bf16[264,768]{1,0:T(8,128)(2,1)S(1)} %get-tuple-element.228), channel_id=1, source_target_pairs={{0,3},{1,2},{2,1},{3,0},{4,7},{5,6},{6,5},{7,4},{8,11},{9,10},{10,... | collective-permute-start | bytes 1216520 | tf_op jit(solution)/shard_map/ppermute | solution.py:29
  385.1 23.7 %collective-permute-start.13 = (bf16[264,768]{1,0:T(8,128)(2,1)S(1)}, bf16[264,768]{1,0:T(8,128)(2,1)S(1)}, u32[]{:S(2)}, u32[]{:S(2)}) collective-permute-start(bf16[264,768]{1,0:T(8,128)(2,1)S(1)} %get-tuple-element.227), channel_id=1, source_target_pairs={{0,1},{1,0},{2,3},{3,2},{4,5},{5,4},{6,7},{7,6},{8,9},{9,8},{10,11... | collective-permute-start | bytes 1216520 | tf_op jit(solution)/shard_map/ppermute | solution.py:29
  417.9 38.5 %collective-permute-start.21 = (bf16[264,768]{1,0:T(8,128)(2,1)S(1)}, bf16[264,768]{1,0:T(8,128)(2,1)S(1)}, u32[]{:S(2)}, u32[]{:S(2)}) collective-permute-start(bf16[264,768]{1,0:T(8,128)(2,1)S(1)} %fusion.149), channel_id=1, source_target_pairs={{0,3},{1,2},{2,1},{3,0},{4,7},{5,6},{6,5},{7,4},{8,11},{9,10},{10,... | collective-permute-start | bytes 1216520 | tf_op jit(solution)/shard_map/ppermute | solution.py:29
  421.5 34.8 %collective-permute-start.20 = (bf16[264,768]{1,0:T(8,128)(2,1)S(1)}, bf16[264,768]{1,0:T(8,128)(2,1)S(1)}, u32[]{:S(2)}, u32[]{:S(2)}) collective-permute-start(bf16[264,768]{1,0:T(8,128)(2,1)S(1)} %fusion.148), channel_id=1, source_target_pairs={{0,2},{1,3},{2,0},{3,1},{4,6},{5,7},{6,4},{7,5},{8,10},{9,11},{10,... | collective-permute-start | bytes 1216520 | tf_op jit(solution)/shard_map/ppermute | solution.py:29
  424.7 46.2 %collective-permute-start.18 = (bf16[264,768]{1,0:T(8,128)(2,1)S(1)}, bf16[264,768]{1,0:T(8,128)(2,1)S(1)}, u32[]{:S(2)}, u32[]{:S(2)}) collective-permute-start(bf16[264,768]{1,0:T(8,128)(2,1)S(1)} %fusion.147), channel_id=1, source_target_pairs={{0,1},{1,0},{2,3},{3,2},{4,5},{5,4},{6,7},{7,6},{8,9},{9,8},{10,11... | collective-permute-start | bytes 1216520 | tf_op jit(solution)/shard_map/ppermute | solution.py:29
  468.3 28.7 %collective-permute-start.22 = (bf16[264,768]{1,0:T(8,128)(2,1)S(1)}, bf16[264,768]{1,0:T(8,128)(2,1)S(1)}, u32[]{:S(2)}, u32[]{:S(2)}) collective-permute-start(bf16[264,768]{1,0:T(8,128)(2,1)S(1)} %get-tuple-element.224), channel_id=1, source_target_pairs={{0,2},{1,3},{2,0},{3,1},{4,6},{5,7},{6,4},{7,5},{8,10},{9,11},{10,... | collective-permute-start | bytes 1216520 | tf_op jit(solution)/shard_map/ppermute | solution.py:29
  468.4 28.6 %collective-permute-start.23 = (bf16[264,768]{1,0:T(8,128)(2,1)S(1)}, bf16[264,768]{1,0:T(8,128)(2,1)S(1)}, u32[]{:S(2)}, u32[]{:S(2)}) collective-permute-start(bf16[264,768]{1,0:T(8,128)(2,1)S(1)} %get-tuple-element.225), channel_id=1, source_target_pairs={{0,3},{1,2},{2,1},{3,0},{4,7},{5,6},{6,5},{7,4},{8,11},{9,10},{10,... | collective-permute-start | bytes 1216520 | tf_op jit(solution)/shard_map/ppermute | solution.py:29
  483.4 22.2 %collective-permute-start.19 = (bf16[264,768]{1,0:T(8,128)(2,1)S(1)}, bf16[264,768]{1,0:T(8,128)(2,1)S(1)}, u32[]{:S(2)}, u32[]{:S(2)}) collective-permute-start(bf16[264,768]{1,0:T(8,128)(2,1)S(1)} %get-tuple-element.223), channel_id=1, source_target_pairs={{0,1},{1,0},{2,3},{3,2},{4,5},{5,4},{6,7},{7,6},{8,9},{9,8},{10,11... | collective-permute-start | bytes 1216520 | tf_op jit(solution)/shard_map/ppermute | solution.py:29
  547.4 23.2 %collective-permute-start.24 = (bf16[264,768]{1,0:T(8,128)(2,1)}, bf16[264,768]{1,0:T(8,128)(2,1)}, u32[]{:S(2)}, u32[]{:S(2)}) collective-permute-start(bf16[264,768]{1,0:T(8,128)(2,1)} %fusion.151), channel_id=1, source_target_pairs={{0,1},{1,0},{2,3},{3,2},{4,5},{5,4},{6,7},{7,6},{8,9},{9,8},{10,11... | collective-permute-start | bytes 1216520 | tf_op jit(solution)/shard_map/ppermute | solution.py:29
  571.8 297.6 %reduce-scatter.6.cloned.1.call-start = ((), (), s32[]{:S(2)}) async-start(), calls=%async_computation.8 | async-start | bytes 15925248 | tf_op jit(solution)/shard_map/reduce_scatter | solution.py:362
  571.8 29.8 %collective-permute-start.26 = (bf16[264,768]{1,0:T(8,128)(2,1)}, bf16[264,768]{1,0:T(8,128)(2,1)S(1)}, u32[]{:S(2)}, u32[]{:S(2)}) collective-permute-start(bf16[264,768]{1,0:T(8,128)(2,1)} %fusion.152), channel_id=1, source_target_pairs={{0,2},{1,3},{2,0},{3,1},{4,6},{5,7},{6,4},{7,5},{8,10},{9,11},{10,... | collective-permute-start | bytes 1216520 | tf_op jit(solution)/shard_map/ppermute | solution.py:29
  573.9 27.7 %collective-permute-start.27 = (bf16[264,768]{1,0:T(8,128)(2,1)}, bf16[264,768]{1,0:T(8,128)(2,1)S(1)}, u32[]{:S(2)}, u32[]{:S(2)}) collective-permute-start(bf16[264,768]{1,0:T(8,128)(2,1)} %fusion.153), channel_id=1, source_target_pairs={{0,3},{1,2},{2,1},{3,0},{4,7},{5,6},{6,5},{7,4},{8,11},{9,10},{10,... | collective-permute-start | bytes 1216520 | tf_op jit(solution)/shard_map/ppermute | solution.py:29
  612.2 36.9 %collective-permute-start.28 = (bf16[264,768]{1,0:T(8,128)(2,1)S(1)}, bf16[264,768]{1,0:T(8,128)(2,1)S(1)}, u32[]{:S(2)}, u32[]{:S(2)}) collective-permute-start(bf16[264,768]{1,0:T(8,128)(2,1)S(1)} %get-tuple-element.220), channel_id=1, source_target_pairs={{0,2},{1,3},{2,0},{3,1},{4,6},{5,7},{6,4},{7,5},{8,10},{9,11},{10,... | collective-permute-start | bytes 1216520 | tf_op jit(solution)/shard_map/ppermute | solution.py:29
  621.5 27.7 %collective-permute-start.29 = (bf16[264,768]{1,0:T(8,128)(2,1)S(1)}, bf16[264,768]{1,0:T(8,128)(2,1)S(1)}, u32[]{:S(2)}, u32[]{:S(2)}) collective-permute-start(bf16[264,768]{1,0:T(8,128)(2,1)S(1)} %get-tuple-element.221), channel_id=1, source_target_pairs={{0,3},{1,2},{2,1},{3,0},{4,7},{5,6},{6,5},{7,4},{8,11},{9,10},{10,... | collective-permute-start | bytes 1216520 | tf_op jit(solution)/shard_map/ppermute | solution.py:29
  633.1 24.2 %collective-permute-start.25 = (bf16[264,768]{1,0:T(8,128)(2,1)S(1)}, bf16[264,768]{1,0:T(8,128)(2,1)S(1)}, u32[]{:S(2)}, u32[]{:S(2)}) collective-permute-start(bf16[264,768]{1,0:T(8,128)(2,1)S(1)} %get-tuple-element.219), channel_id=1, source_target_pairs={{0,1},{1,0},{2,3},{3,2},{4,5},{5,4},{6,7},{7,6},{8,9},{9,8},{10,11... | collective-permute-start | bytes 1216520 | tf_op jit(solution)/shard_map/ppermute | solution.py:29
  691.8 29.1 %collective-permute-start.30 = (bf16[264,768]{1,0:T(8,128)(2,1)S(1)}, bf16[264,768]{1,0:T(8,128)(2,1)S(1)}, u32[]{:S(2)}, u32[]{:S(2)}) collective-permute-start(bf16[264,768]{1,0:T(8,128)(2,1)S(1)} %fusion.155), channel_id=1, source_target_pairs={{0,1},{1,0},{2,3},{3,2},{4,5},{5,4},{6,7},{7,6},{8,9},{9,8},{10,11... | collective-permute-start | bytes 1216520 | tf_op jit(solution)/shard_map/ppermute | solution.py:29
  721.1 238.2 %reduce-scatter.8.cloned.1.call-start = ((), (), s32[]{:S(2)}) async-start(), calls=%async_computation.9 | async-start | bytes 10616832 | tf_op jit(solution)/shard_map/reduce_scatter | solution.py:362
  727.0 37.5 %collective-permute-start.33 = (bf16[264,768]{1,0:T(8,128)(2,1)}, bf16[264,768]{1,0:T(8,128)(2,1)S(1)}, u32[]{:S(2)}, u32[]{:S(2)}) collective-permute-start(bf16[264,768]{1,0:T(8,128)(2,1)} %fusion.157), channel_id=1, source_target_pairs={{0,3},{1,2},{2,1},{3,0},{4,7},{5,6},{6,5},{7,4},{8,11},{9,10},{10,... | collective-permute-start | bytes 1216520 | tf_op jit(solution)/shard_map/ppermute | solution.py:29
  729.2 35.3 %collective-permute-start.32 = (bf16[264,768]{1,0:T(8,128)(2,1)}, bf16[264,768]{1,0:T(8,128)(2,1)S(1)}, u32[]{:S(2)}, u32[]{:S(2)}) collective-permute-start(bf16[264,768]{1,0:T(8,128)(2,1)} %fusion.156), channel_id=1, source_target_pairs={{0,2},{1,3},{2,0},{3,1},{4,6},{5,7},{6,4},{7,5},{8,10},{9,11},{10,... | collective-permute-start | bytes 1216520 | tf_op jit(solution)/shard_map/ppermute | solution.py:29
  777.1 28.3 %collective-permute-start.34 = (bf16[264,768]{1,0:T(8,128)(2,1)S(1)}, bf16[264,768]{1,0:T(8,128)(2,1)S(1)}, u32[]{:S(2)}, u32[]{:S(2)}) collective-permute-start(bf16[264,768]{1,0:T(8,128)(2,1)S(1)} %get-tuple-element.216), channel_id=1, source_target_pairs={{0,2},{1,3},{2,0},{3,1},{4,6},{5,7},{6,4},{7,5},{8,10},{9,11},{10,... | collective-permute-start | bytes 1216520 | tf_op jit(solution)/shard_map/ppermute | solution.py:29
  777.1 28.3 %collective-permute-start.35 = (bf16[264,768]{1,0:T(8,128)(2,1)S(1)}, bf16[264,768]{1,0:T(8,128)(2,1)S(1)}, u32[]{:S(2)}, u32[]{:S(2)}) collective-permute-start(bf16[264,768]{1,0:T(8,128)(2,1)S(1)} %get-tuple-element.217), channel_id=1, source_target_pairs={{0,3},{1,2},{2,1},{3,0},{4,7},{5,6},{6,5},{7,4},{8,11},{9,10},{10,... | collective-permute-start | bytes 1216520 | tf_op jit(solution)/shard_map/ppermute | solution.py:29
  792.4 34.1 %collective-permute-start.31 = (bf16[264,768]{1,0:T(8,128)(2,1)}, bf16[264,768]{1,0:T(8,128)(2,1)}, u32[]{:S(2)}, u32[]{:S(2)}) collective-permute-start(bf16[264,768]{1,0:T(8,128)(2,1)} %get-tuple-element.215), channel_id=1, source_target_pairs={{0,1},{1,0},{2,3},{3,2},{4,5},{5,4},{6,7},{7,6},{8,9},{9,8},{10,11... | collective-permute-start | bytes 1216520 | tf_op jit(solution)/shard_map/ppermute | solution.py:29
  861.5 4.9 collective-permute-start.36
  871.5 16.9 %collective-permute-start.37 = (bf16[1,2,4,96,384]{4,3,2,1,0:T(8,128)(2,1)}, bf16[1,2,4,96,384]{4,3,2,1,0:T(8,128)(2,1)}, u32[]{:S(2)}, u32[]{:S(2)}) collective-permute-start(bf16[1,2,4,96,384]{4,3,2,1,0:T(8,128)(2,1)} %dynamic-slice_bitcast_fusion.2), channel_id=1, source_target_pairs={{0,8},{4,12},{8,0},{12,4},{16,24},{20,28},{24,16},{28,20},{1,9},{5... | collective-permute-start | bytes 1769480 | tf_op jit(solution)/shard_map/ppermute | solution.py:29
  877.2 35.8 %collective-permute-start.43 = (bf16[2,192,768]{2,1,0:T(8,128)(2,1)}, bf16[2,192,768]{2,1,0:T(8,128)(2,1)}, u32[]{:S(2)}, u32[]{:S(2)}) collective-permute-start(bf16[2,192,768]{2,1,0:T(8,128)(2,1)} %dynamic-slice_bitcast_fusion.1), channel_id=1, source_target_pairs={{0,2},{1,3},{2,0},{3,1},{4,6},{5,7},{6,4},{7,5},{8,10},{9,11},{10,... | collective-permute-start | bytes 1769480 | tf_op jit(solution)/shard_map/ppermute | solution.py:29
  887.9 26.3 %collective-permute-start.39 = (bf16[1,2,4,104,384]{4,3,2,1,0:T(8,128)(2,1)S(1)}, bf16[1,2,4,104,384]{4,3,2,1,0:T(8,128)(2,1)}, u32[]{:S(2)}, u32[]{:S(2)}) collective-permute-start(bf16[1,2,4,104,384]{4,3,2,1,0:T(8,128)(2,1)S(1)} %dynamic-slice_bitcast_fusion), channel_id=1, source_target_pairs={{0,16},{4,20},{8,24},{12,28},{16,0},{20,4},{24,8},{28,12},{1,17},{... | collective-permute-start | bytes 1916936 | tf_op jit(solution)/shard_map/ppermute | solution.py:29
  890.2 27.5 %collective-permute-start.38 = (bf16[1,1,4,96,384]{4,3,2,1,0:T(8,128)(2,1)S(1)}, bf16[1,1,4,96,384]{4,3,2,1,0:T(8,128)(2,1)S(1)}, u32[]{:S(2)}, u32[]{:S(2)}) collective-permute-start(bf16[1,1,4,96,384]{4,3,2,1,0:T(8,128)(2,1)S(1)} %constant_dynamic-slice_fusion.3), channel_id=1, source_target_pairs={{0,16},{4,20},{8,24},{12,28},{16,0},{20,4},{24,8},{28,12},{1,17},{... | collective-permute-start | bytes 884744 | tf_op jit(solution)/shard_map/ppermute | solution.py:29
  915.7 16.8 %collective-permute-start.40 = (bf16[1,1,4,104,384]{4,3,2,1,0:T(8,128)(2,1)S(1)}, bf16[1,1,4,104,384]{4,3,2,1,0:T(8,128)(2,1)S(1)}, u32[]{:S(2)}, u32[]{:S(2)}) collective-permute-start(bf16[1,1,4,104,384]{4,3,2,1,0:T(8,128)(2,1)S(1)} %constant_dynamic-slice_fusion.2), channel_id=1, source_target_pairs={{0,8},{4,12},{8,0},{12,4},{16,24},{20,28},{24,16},{28,20},{1,9},{5... | collective-permute-start | bytes 958472 | tf_op jit(solution)/shard_map/ppermute | solution.py:29
  916.9 18.7 %collective-permute-start.44 = (bf16[1,192,768]{2,1,0:T(8,128)(2,1)}, bf16[1,192,768]{2,1,0:T(8,128)(2,1)}, u32[]{:S(2)}, u32[]{:S(2)}) collective-permute-start(bf16[1,192,768]{2,1,0:T(8,128)(2,1)} %constant_dynamic-slice_fusion), channel_id=1, source_target_pairs={{0,1},{1,0},{2,3},{3,2},{4,5},{5,4},{6,7},{7,6},{8,9},{9,8},{10,11... | collective-permute-start | bytes 884744 | tf_op jit(solution)/shard_map/ppermute | solution.py:29
  932.7 14.8 %collective-permute-start.41 = (bf16[2,200,384]{2,1,0:T(8,128)(2,1)S(1)}, bf16[2,200,384]{2,1,0:T(8,128)(2,1)}, u32[]{:S(2)}, u32[]{:S(2)}) collective-permute-start(bf16[2,200,384]{2,1,0:T(8,128)(2,1)S(1)} %fusion.228), channel_id=1, source_target_pairs={{0,2},{1,3},{2,0},{3,1},{4,6},{5,7},{6,4},{7,5},{8,10},{9,11},{10,... | collective-permute-start | bytes 921608 | tf_op jit(solution)/shard_map/ppermute | solution.py:29
  948.6 6.0 collective-permute-start.42
  964.1 7.1 collective-permute-start.45
  965.7 7.1 collective-permute-start.47
  971.3 10.9 %collective-permute-start.46 = (bf16[1,2,288,384]{3,2,1,0:T(8,128)(2,1)S(1)}, bf16[1,2,288,384]{3,2,1,0:T(8,128)(2,1)S(1)}, u32[]{:S(2)}, u32[]{:S(2)}) collective-permute-start(bf16[1,2,288,384]{3,2,1,0:T(8,128)(2,1)S(1)} %fusion.240), channel_id=1, source_target_pairs={{0,8},{4,12},{8,0},{12,4},{16,24},{20,28},{24,16},{28,20},{1,9},{5... | collective-permute-start | bytes 1327112 | tf_op jit(solution)/shard_map/ppermute | solution.py:29
  972.9 10.9 %collective-permute-start.48 = (bf16[1,2,296,384]{3,2,1,0:T(8,128)(2,1)S(1)}, bf16[1,2,296,384]{3,2,1,0:T(8,128)(2,1)S(1)}, u32[]{:S(2)}, u32[]{:S(2)}) collective-permute-start(bf16[1,2,296,384]{3,2,1,0:T(8,128)(2,1)S(1)} %fusion.239), channel_id=1, source_target_pairs={{0,16},{4,20},{8,24},{12,28},{16,0},{20,4},{24,8},{28,12},{1,17},{... | collective-permute-start | bytes 1363976 | tf_op jit(solution)/shard_map/ppermute | solution.py:29
  984.3 3.8 collective-permute-start.49
  (142 other events, 2935.8 us)
Sparse Core Ops, SparseCore 0:
  33.2 37.8 all-gather.6
  93.4 39.2 all-gather.8
  214.7 36.9 all-gather.10
  571.9 99.9 reduce-scatter.3
  721.2 100.6 reduce-scatter.5
  869.5 89.6 reduce-scatter.7
where the time goes:
time: 1010 us; the launch traced here: 1000 us
  waiting for transfers between devices  359 us (36%)
  matrix products  209 us (21%)
  Pallas kernels  184 us (18%)
  starting transfers between devices  104 us (10%)
  other arithmetic  50.5 us (5%)
  local copies, waits for them, and re-layouts  42.8 us (4%)
  blocking collectives  35.3 us (3%)
  between operations  17.6 us (2%)
    ppermute x50, waiting for transfers between devices, swap(): return lax.ppermute(values, axis, [(n, n ^ bit) for n in range(count)])  330 us
    dot_general x51, matrix products, dot_on(): lax.dot_general(left, right, (((left_axis,), (right_axis,)), ((), ())), p...  122 us
    ppermute x50, starting transfers between devices, swap(): return lax.ppermute(values, axis, [(n, n ^ bit) for n in range(count)])  94.8 us
    pallas_call x3, Pallas kernels, attention_backward(): pl.pallas_call(functools.partial(attention_back_kernel, length), grid=(im...  86 us
    pallas_call x3, Pallas kernels, expert_grads(): pl.pallas_call(kernel, grid=(hidden // block,), in_specs=cut_spec + full_...  57.8 us
    dot_general x6, matrix products, expert_forward(): pre_act = jnp.dot(arrived, first_weight, preferred_element_type=f32)  49.2 us
    pallas_call x3, Pallas kernels, attention_forward(): pl.pallas_call(functools.partial(attention_kernel, length), grid=(images,...  33.3 us
    unnamed x317, local copies, waits for them, and re-layouts  22.5 us
  transfers between devices with their start and end apart: 58, of which 29 were waited for; matrix products, arithmetic and copies ran while one was open for 25% of the time, Pallas kernels for 14%

commit v1 on v0

--- a/solution.py
+++ b/solution.py
@@ -46,7 +46,7 @@
     return bits, bits[::-1]
 
 
-def add_swapped(values, axis, bit, size, at):
+def add_swapped(values, axis, bit, size, at, hold=None):
     lead, rows, rest = values.shape[:at], values.shape[at], values.shape[at + 1 :]
     view = values.reshape(lead + (rows // (2 * size), 2, size) + rest)
     own = bit_of(axis, bit).astype(jnp.int32)
@@ -54,6 +54,8 @@
     sent = lax.dynamic_index_in_dim(view, 1 - own, at + 1, keepdims=False)
     shape = lead + (rows // 2,) + rest
     arrived = swap(sent.reshape(shape), axis, bit)
+    if hold is not None:
+        kept = after(kept, hold)
     return (kept.reshape(shape).astype(f32) + arrived.astype(f32)).astype(bf16)
 
 
@@ -107,14 +109,14 @@
     return lax.optimization_barrier((values,) + others)[0]
 
 
-def gather_shard(packed):
-    rows, columns = packed.shape
-    width = columns // lax.axis_size("replica")
-    own = lax.dynamic_slice_in_dim(packed, lax.axis_index("replica") * width, width, axis=1)
-    shards_ = lax.axis_size("shard")
-    spread = jnp.broadcast_to(own[None], (shards_, rows, width))
-    tall = lax.all_to_all(spread, "shard", split_axis=0, concat_axis=0, tiled=True)
-    return tall.reshape(shards_ * rows, width)
+def own_columns(packed):
+    width = packed.shape[-1] // lax.axis_size("replica")
+    return lax.dynamic_slice_in_dim(packed, lax.axis_index("replica") * width, width, axis=packed.ndim - 1)
+
+
+def gather_shard(own):
+    spread = jnp.broadcast_to(own[None], (lax.axis_size("shard"),) + own.shape)
+    return lax.all_to_all(spread, "shard", split_axis=0, concat_axis=0, tiled=True)
 
 
 def split_sum(summed, features):
@@ -549,7 +551,10 @@
         jnp.transpose(router_weight, (0, 2, 1)).reshape(LAYERS * experts, -1), "shard", axis=1, tiled=True
     ).reshape(LAYERS, experts, features)
     router_all = jnp.pad(router_all, ((0, 0), (0, -experts % 8), (0, 0)))
-    weight = lax.all_gather(gather_shard(packed[0]), "replica", axis=0, tiled=False)
+    own = own_columns(packed)
+    first = gather_shard(own[0]).reshape(features, -1)
+    later = gather_shard(after(own[1:], first))
+    weight = lax.all_gather(first, "replica", axis=0, tiled=False)
     ids_flat = expert_ids.reshape(-1)
     labels = jnp.arange(experts, dtype=jnp.int32)
     member = (ids_flat[:, None] == labels[None, :]).astype(jnp.int32)
@@ -566,20 +571,23 @@
         singles = [(at[:, k : k + 1] == slot_row).astype(bf16) for k in range(2)]
         places[j] = (singles[0] + singles[1], singles)
     residual = jnp.pad(tokens, fill).astype(f32)
+    gradient = jnp.pad(cotangent, fill).astype(f32)
+    weight, later, places, choose, gradient = lax.optimization_barrier(
+        (weight, later, places, choose, gradient)
+    )
     records = []
     weights = []
     for index in range(LAYERS):
         weights.append(weight)
         tall = None
         if index + 1 < LAYERS:
-            tall = gather_shard(after(packed[index + 1], weight))
+            tall = later[:, index].reshape(features, -1)
         record, residual, weight = forward_layer(
             residual, weight, router_all[index], norm_gain[index], norm_shift[index],
             expert_in[index, 0], expert_out[index, 0], choose, places, length, tall,
         )
         records.append(record)
     activations = residual[:, :length].astype(bf16)
-    gradient = jnp.pad(cotangent, fill).astype(f32)
     items = [None] * LAYERS
     grad_weight, terms, summed = None, None, ()
     wide = 2 * (expert_in.shape[3] // replicas) == features and features % (4 * features // replicas) == 0
@@ -604,7 +612,7 @@
     upper_dense = jnp.concatenate([part[1] for part in upper], axis=1)
     upper_dense = upper_dense.reshape(experts, -1, upper_dense.shape[1])
     for bit in bits_from("shard", 1)[::-1]:
-        upper_dense = add_swapped(upper_dense, "shard", bit, bit, 0)
+        upper_dense = add_swapped(upper_dense, "shard", bit, bit, 0, whole)
     upper_dense = upper_dense[0]
     own_sum = sum_replica(after(own_grads, summed))
     for bit in bits_from("shard", 1)[::-1]:

time: 1010 us -> 967 us (0.957)
  matrix products: 209 us -> 168 us
  blocking collectives: 35.3 us -> 55.3 us
    dot_general x51, matrix products: 122 us -> 89.2 us  [dot_on(): lax.dot_general(left, right, (((left_axis,), (right_axis,)), ((), ())), p...]
    all_gather x1, waiting for transfers between devices: 20.3 us -> 0.01 us  [shards(): weight = lax.all_gather(first, 'replica', axis=0, tiled=False)]
    all_gather x1, blocking collectives: 13.1 us -> 33.2 us  [shards(): lax.all_gather(jnp.transpose(router_weight, (0, 2, 1)).reshape(LAYERS * e...]
    ppermute x50, waiting for transfers between devices: 330 us -> 344 us  [swap(): return lax.ppermute(values, axis, [(n, n ^ bit) for n in range(count)])]
    unnamed x317 -> x356, local copies, waits for them, and re-layouts: 22.5 us -> 24.8 us
  transfers between devices with their start and end apart: 58 -> 57, of which waited for: 29 -> 27; matrix products, arithmetic and copies ran while one was open for 25% -> 22% of each run, Pallas kernels for 14% -> 12%
where the time goes in v1:
time: 967 us; the launch traced here: 960 us
  waiting for transfers between devices  352 us (36%)
  Pallas kernels  184 us (19%)
  matrix products  168 us (17%)
  starting transfers between devices  98.2 us (10%)
  blocking collectives  55.3 us (6%)
  other arithmetic  45.6 us (5%)
  local copies, waits for them, and re-layouts  38.9 us (4%)
  between operations  17.7 us (2%)
    ppermute x50, waiting for transfers between devices, swap(): return lax.ppermute(values, axis, [(n, n ^ bit) for n in range(count)])  344 us
    ppermute x50, starting transfers between devices, swap(): return lax.ppermute(values, axis, [(n, n ^ bit) for n in range(count)])  94.3 us
    dot_general x51, matrix products, dot_on(): lax.dot_general(left, right, (((left_axis,), (right_axis,)), ((), ())), p...  89.2 us
    pallas_call x3, Pallas kernels, attention_backward(): pl.pallas_call(functools.partial(attention_back_kernel, length), grid=(im...  85.3 us
    pallas_call x3, Pallas kernels, expert_grads(): pl.pallas_call(kernel, grid=(hidden // block,), in_specs=cut_spec + full_...  57.9 us
    dot_general x6, matrix products, expert_forward(): pre_act = jnp.dot(arrived, first_weight, preferred_element_type=f32)  39.8 us
    pallas_call x3, Pallas kernels, attention_forward(): pl.pallas_call(functools.partial(attention_kernel, length), grid=(images,...  34 us
    all_gather x1, blocking collectives, shards(): lax.all_gather(jnp.transpose(router_weight, (0, 2, 1)).reshape(LAYERS * e...  33.2 us
  transfers between devices with their start and end apart: 57, of which 27 were waited for; matrix products, arithmetic and copies ran while one was open for 22% of the time, Pallas kernels for 12%

profile of v1, /device:TPU:0, one launch (start us, length us, event | category | flops | bytes accessed | tf_op | source)
XLA Modules:
  0.0 959.5 jit_solution(15469785236331215766)
XLA Ops:
  8.5 22.1 %all_to_all.10 = bf16[4,192,384]{2,1,0:T(8,128)(2,1)} all-to-all(bf16[4,192,384]{2,1,0:T(8,128)(2,1)S(1)} %broadcast_in_dim.20), channel_id=1, replica_groups=mesh['replica'=8,'shard'=4] {'shard'}, dimensions={0} | all-to-all | bytes 1179648 | tf_op jit(solution)/shard_map/all_to_all | solution.py:119
  31.9 3.5 all-to-all-start.1
  35.8 33.2 %all-gather.2 = bf16[4,192,12]{1,2,0:T(8,128)(2,1)S(1)} all-gather(bf16[1,192,12]{1,2,0:T(8,128)(2,1)S(1)} %bitcast.455), channel_id=1, replica_groups=mesh['replica'=8,'shard'=4] {'shard'}, dimensions={0}, use_global_device_ids=true | all-gather | bytes 23040 | tf_op jit(solution)/shard_map/all_gather | solution.py:550
  86.5 11.0 %attention_forward.3 = (bf16[2,208,2304]{2,1,0:T(8,128)(2,1)S(1)}, bf16[2,208,768]{2,1,0:T(8,128)(2,1)S(1)}, f32[2,208,768]{2,1,0:T(8,128)S(1)}, bf16[2,208,768]{2,1,0:T(8,128)(2,1)S(1)}, f32[2,208,8]{2,1,0:T(8,128)S(1)}) custom-call(f32[2,208,768]{2,1,0:T(8,128)S(1)} %pad_convert_fusion.1.res_ref, bf16[8,768,384]{2,1,0:T(8,128)(2,1)} %all-gather.7.cloned.1.call-done.w_ref, ...), custom_call_target="tpu_custom_call" | custom-call | tf_op jit(solution)/shard_map/attention_forward/pallas_call | solution.py:188
  110.7 24.0 %collective-permute-done.2 = bf16[264,768]{1,0:T(8,128)(2,1)S(1)} collective-permute-done((bf16[264,768]{1,0:T(8,128)(2,1)S(1)}, bf16[264,768]{1,0:T(8,128)(2,1)S(1)}, u32[]{:S(2)}, u32[]{:S(2)}) %collective-permute-start.2) | collective-permute-done | bytes 405536 | tf_op jit(solution)/shard_map/ppermute | solution.py:29
  134.8 6.7 multiply_convert_fusion.10
  148.1 5.4 collective-permute-start.4
  153.5 6.6 multiply_convert_fusion.11
  163.0 18.7 %collective-permute-done.4 = bf16[264,768]{1,0:T(8,128)(2,1)S(1)} collective-permute-done((bf16[264,768]{1,0:T(8,128)(2,1)S(1)}, bf16[264,768]{1,0:T(8,128)(2,1)S(1)}, u32[]{:S(2)}, u32[]{:S(2)}) %collective-permute-start.4) | collective-permute-done | bytes 405536 | tf_op jit(solution)/shard_map/ppermute | solution.py:29
  185.9 11.4 %attention_forward.4 = (bf16[2,208,2304]{2,1,0:T(8,128)(2,1)S(1)}, bf16[2,208,768]{2,1,0:T(8,128)(2,1)S(1)}, f32[2,208,768]{2,1,0:T(8,128)S(1)}, bf16[2,208,768]{2,1,0:T(8,128)(2,1)S(1)}, f32[2,208,8]{2,1,0:T(8,128)S(1)}) custom-call(f32[2,208,768]{2,1,0:T(8,128)S(1)} %add.263.res_ref, bf16[8,768,384]{2,1,0:T(8,128)(2,1)} %bitcast.414, ...), custom_call_target="tpu_custom_call" | custom-call | tf_op jit(solution)/shard_map/attention_forward/pallas_call | solution.py:188
  209.1 20.9 %collective-permute-done.8 = bf16[264,768]{1,0:T(8,128)(2,1)S(1)} collective-permute-done((bf16[264,768]{1,0:T(8,128)(2,1)S(1)}, bf16[264,768]{1,0:T(8,128)(2,1)S(1)}, u32[]{:S(2)}, u32[]{:S(2)}) %collective-permute-start.8) | collective-permute-done | bytes 405536 | tf_op jit(solution)/shard_map/ppermute | solution.py:29
  230.2 6.8 multiply_convert_fusion.8
  243.7 8.2 collective-permute-start.10
  251.9 6.6 multiply_convert_fusion.9
  258.5 2.7 fusion.127
  261.4 19.4 %collective-permute-done.10 = bf16[264,768]{1,0:T(8,128)(2,1)S(1)} collective-permute-done((bf16[264,768]{1,0:T(8,128)(2,1)S(1)}, bf16[264,768]{1,0:T(8,128)(2,1)S(1)}, u32[]{:S(2)}, u32[]{:S(2)}) %collective-permute-start.10) | collective-permute-done | bytes 405536 | tf_op jit(solution)/shard_map/ppermute | solution.py:29
  285.0 11.6 %attention_forward.5 = (bf16[2,208,2304]{2,1,0:T(8,128)(2,1)S(1)}, bf16[2,208,768]{2,1,0:T(8,128)(2,1)S(1)}, f32[2,208,768]{2,1,0:T(8,128)S(1)}, bf16[2,208,768]{2,1,0:T(8,128)(2,1)S(1)}, f32[2,208,8]{2,1,0:T(8,128)S(1)}) custom-call(f32[2,208,768]{2,1,0:T(8,128)S(1)} %add.269.res_ref, bf16[8,768,384]{2,1,0:T(8,128)(2,1)} %bitcast.416, ...), custom_call_target="tpu_custom_call" | custom-call | tf_op jit(solution)/shard_map/attention_forward/pallas_call | solution.py:188
  302.4 24.5 %collective-permute-done.14 = bf16[264,768]{1,0:T(8,128)(2,1)S(1)} collective-permute-done((bf16[264,768]{1,0:T(8,128)(2,1)S(1)}, bf16[264,768]{1,0:T(8,128)(2,1)S(1)}, u32[]{:S(2)}, u32[]{:S(2)}) %collective-permute-start.14) | collective-permute-done | bytes 405536 | tf_op jit(solution)/shard_map/ppermute | solution.py:29
  327.1 6.6 multiply_convert_fusion.6
  337.5 9.6 %collective-permute-start.16 = (bf16[264,768]{1,0:T(8,128)(2,1)S(1)}, bf16[264,768]{1,0:T(8,128)(2,1)S(1)}, u32[]{:S(2)}, u32[]{:S(2)}) collective-permute-start(bf16[264,768]{1,0:T(8,128)(2,1)S(1)} %get-tuple-element.261), channel_id=1, source_target_pairs={{0,2},{1,3},{2,0},{3,1},{4,6},{5,7},{6,4},{7,5},{8,10},{9,11},{10,... | collective-permute-start | bytes 1216520 | tf_op jit(solution)/shard_map/ppermute | solution.py:29
  347.2 6.6 multiply_convert_fusion.7
  358.6 16.2 %collective-permute-done.16 = bf16[264,768]{1,0:T(8,128)(2,1)S(1)} collective-permute-done((bf16[264,768]{1,0:T(8,128)(2,1)S(1)}, bf16[264,768]{1,0:T(8,128)(2,1)S(1)}, u32[]{:S(2)}, u32[]{:S(2)}) %collective-permute-start.16) | collective-permute-done | bytes 405536 | tf_op jit(solution)/shard_map/ppermute | solution.py:29
  376.4 6.4 collective-permute-done.13
  394.8 32.2 %collective-permute-done.20 = bf16[264,768]{1,0:T(8,128)(2,1)S(1)} collective-permute-done((bf16[264,768]{1,0:T(8,128)(2,1)S(1)}, bf16[264,768]{1,0:T(8,128)(2,1)S(1)}, u32[]{:S(2)}, u32[]{:S(2)}) %collective-permute-start.20) | collective-permute-done | bytes 405536 | tf_op jit(solution)/shard_map/ppermute | solution.py:29
  427.1 7.3 multiply_convert_fusion.4.refs_1_
  434.5 2.7 fusion.136
  439.4 6.8 multiply_convert_fusion.5.refs_0_
  446.2 2.7 fusion.133
  451.0 14.6 %collective-permute-done.22 = bf16[264,768]{1,0:T(8,128)(2,1)S(1)} collective-permute-done((bf16[264,768]{1,0:T(8,128)(2,1)S(1)}, bf16[264,768]{1,0:T(8,128)(2,1)S(1)}, u32[]{:S(2)}, u32[]{:S(2)}) %collective-permute-start.22) | collective-permute-done | bytes 405536 | tf_op jit(solution)/shard_map/ppermute | solution.py:29
  466.3 7.8 collective-permute-done.19
  475.9 28.6 %attention_backward.3 = (f32[2,208,768]{2,1,0:T(8,128)}, bf16[8,768,1152]{2,1,0:T(8,128)(2,1)}, f32[8,768]{1,0:T(8,128)}) custom-call(f32[2,208,768]{2,1,0:T(8,128)} %bitcast.427, f32[2,208,768]{2,1,0:T(8,128)} %pad_convert_fusion.grad_ref, f32[2,208,768]{2,1,0:T(8,128)} %copy-done.2, f32[2,208,768]{2,1,0:T(8,128)} %copy-done.7, ...), custom_call_target="tpu_custom_call" | custom-call | tf_op jit(solution)/shard_map/attention_backward/pallas_call | solution.py:297
  514.1 19.3 %expert_grads.3 = bf16[8,768,1152]{2,1,0:T(8,128)(2,1)} custom-call(bf16[528,3072]{1,0:T(8,128)(2,1)S(1)} %copy-done.22, bf16[528,3072]{1,0:T(8,128)(2,1)S(1)} %copy-done.18, bf16[528,768]{1,0:T(8,128)(2,1)S(1)} %pad_maximum_fusion.9.refs_2_, bf16[528,768]{1,0:T(8,128)(2,1)S(1)} %constant_dynamic-update-slice_fusion.8.refs_3_, ...), custom_call_target="tpu_custom_call", output_to_operand_aliasing={{}: (8, {})} | custom-call | tf_op jit(solution)/shard_map/expert_grads/pallas_call | solution.py:348
  541.6 22.8 %collective-permute-done.26 = bf16[264,768]{1,0:T(8,128)(2,1)S(1)} collective-permute-done((bf16[264,768]{1,0:T(8,128)(2,1)}, bf16[264,768]{1,0:T(8,128)(2,1)S(1)}, u32[]{:S(2)}, u32[]{:S(2)}) %collective-permute-start.26) | collective-permute-done | bytes 405536 | tf_op jit(solution)/shard_map/ppermute | solution.py:29
  564.5 8.0 multiply_convert_fusion.2.refs_1_
  572.8 2.7 fusion.124
  575.6 8.8 collective-permute-start.28
  586.5 7.2 multiply_convert_fusion.3.refs_0_
  593.7 2.7 fusion.121
  597.3 14.7 %collective-permute-done.28 = bf16[264,768]{1,0:T(8,128)(2,1)S(1)} collective-permute-done((bf16[264,768]{1,0:T(8,128)(2,1)S(1)}, bf16[264,768]{1,0:T(8,128)(2,1)S(1)}, u32[]{:S(2)}, u32[]{:S(2)}) %collective-permute-start.28) | collective-permute-done | bytes 405536 | tf_op jit(solution)/shard_map/ppermute | solution.py:29
  612.7 7.6 collective-permute-done.25
  622.1 28.3 %attention_backward.4 = (f32[2,208,768]{2,1,0:T(8,128)}, bf16[8,768,1152]{2,1,0:T(8,128)(2,1)}, f32[8,768]{1,0:T(8,128)}) custom-call(f32[2,208,768]{2,1,0:T(8,128)} %bitcast.426, f32[2,208,768]{2,1,0:T(8,128)} %get-tuple-element.131.grad_ref, f32[2,208,768]{2,1,0:T(8,128)} %copy-done.1, f32[2,208,768]{2,1,0:T(8,128)} %copy-done.6, ...), custom_call_target="tpu_custom_call" | custom-call | tf_op jit(solution)/shard_map/attention_backward/pallas_call | solution.py:297
  659.5 19.2 %expert_grads.4 = bf16[8,768,1152]{2,1,0:T(8,128)(2,1)} custom-call(bf16[528,3072]{1,0:T(8,128)(2,1)S(1)} %copy-done.20, bf16[528,3072]{1,0:T(8,128)(2,1)S(1)} %multiply_convert_fusion.2.refs_1_, bf16[528,768]{1,0:T(8,128)(2,1)S(1)} %pad_maximum_fusion.7.refs_2_, bf16[528,768]{1,0:T(8,128)(2,1)S(1)} %copy-done.29, ...), custom_call_target="tpu_custom_call", output_to_operand_aliasing={{}: (8, {})} | custom-call | tf_op jit(solution)/shard_map/expert_grads/pallas_call | solution.py:348
  688.9 3.2 multiply_reduce_fusion.1
  695.3 29.1 %collective-permute-done.32 = bf16[264,768]{1,0:T(8,128)(2,1)S(1)} collective-permute-done((bf16[264,768]{1,0:T(8,128)(2,1)}, bf16[264,768]{1,0:T(8,128)(2,1)S(1)}, u32[]{:S(2)}, u32[]{:S(2)}) %collective-permute-start.32) | collective-permute-done | bytes 405536 | tf_op jit(solution)/shard_map/ppermute | solution.py:29
  724.5 7.6 multiply_convert_fusion.refs_1_
  732.2 2.7 fusion.112
  738.0 5.9 multiply_convert_fusion.1.refs_0_
  744.0 2.7 fusion.109
  750.5 13.7 %collective-permute-done.34 = bf16[264,768]{1,0:T(8,128)(2,1)} collective-permute-done((bf16[264,768]{1,0:T(8,128)(2,1)}, bf16[264,768]{1,0:T(8,128)(2,1)}, u32[]{:S(2)}, u32[]{:S(2)}) %collective-permute-start.34) | collective-permute-done | bytes 405536 | tf_op jit(solution)/shard_map/ppermute | solution.py:29
  764.2 3.1 fusion.178
  771.1 19.3 %expert_grads.5 = bf16[8,768,768]{2,1,0:T(8,128)(2,1)} custom-call(bf16[528,3072]{1,0:T(8,128)(2,1)S(1)} %copy-done.14, bf16[528,3072]{1,0:T(8,128)(2,1)S(1)} %copy-done.12, bf16[528,768]{1,0:T(8,128)(2,1)S(1)} %pad_maximum_fusion.5.refs_2_, bf16[528,768]{1,0:T(8,128)(2,1)S(1)} %copy-done.27, bf16[528,3072]{1,0:T(8,128)(2,1)S(1)} %copy-done.10, ...), custom_call_target="tpu_custom_call" | custom-call | tf_op jit(solution)/shard_map/expert_grads/pallas_call | solution.py:348
  794.2 28.4 %attention_backward.5 = (f32[2,208,768]{2,1,0:T(8,128)}, bf16[8,768,384]{2,1,0:T(8,128)(2,1)}, f32[8,768]{1,0:T(8,128)}) custom-call(f32[2,208,768]{2,1,0:T(8,128)} %bitcast.430, f32[2,208,768]{2,1,0:T(8,128)} %get-tuple-element.144.grad_ref, f32[2,208,768]{2,1,0:T(8,128)} %copy-done, f32[2,208,768]{2,1,0:T(8,128)} %copy-done.5, ...), custom_call_target="tpu_custom_call" | custom-call | tf_op jit(solution)/shard_map/attention_backward/pallas_call | solution.py:297
  825.7 4.8 collective-permute-done.36
  830.5 3.0 fusion.30
  841.5 8.8 collective-permute-done.37
  855.0 9.5 collective-permute-start.43
  864.8 24.6 %collective-permute-done.43 = bf16[2,192,768]{2,1,0:T(8,128)(2,1)S(1)} collective-permute-done((bf16[2,192,768]{2,1,0:T(8,128)(2,1)S(1)}, bf16[2,192,768]{2,1,0:T(8,128)(2,1)S(1)}, u32[]{:S(2)}, u32[]{:S(2)}) %collective-permute-start.43) | collective-permute-done | bytes 589856 | tf_op jit(solution)/shard_map/ppermute | solution.py:29
  892.6 10.2 %collective-permute-done.44 = bf16[1,192,768]{2,1,0:T(8,128)(2,1)S(1)} collective-permute-done((bf16[1,192,768]{2,1,0:T(8,128)(2,1)S(1)}, bf16[1,192,768]{2,1,0:T(8,128)(2,1)S(1)}, u32[]{:S(2)}, u32[]{:S(2)}) %collective-permute-start.44) | collective-permute-done | bytes 294944 | tf_op jit(solution)/shard_map/ppermute | solution.py:29
  905.0 5.2 collective-permute-done.42
  910.3 7.0 reduce-scatter.8.cloned.1.call-done
  918.6 3.5 assemble_experts.1
  924.3 4.9 collective-permute-done.45
  931.5 8.7 collective-permute-done.46
  947.3 3.4 assemble.1
  (667 shorter events, 199.3 us)
Async XLA Ops:
  7.2 78.2 %all-gather.7.cloned.1.call-start = ((), (), s32[]{:S(2)}) async-start(), calls=%async_computation.5 | async-start | bytes 5308416 | tf_op jit(solution)/shard_map/all_gather | solution.py:557
  31.9 53.5 %all-to-all-start.1 = ((bf16[4,2,192,384]{3,2,1,0:T(8,128)(2,1)}), bf16[4,2,192,384]{3,2,1,0:T(8,128)(2,1)S(1)}, u32[]{:S(2)}, u32[]{:S(2)}) async-start(bf16[4,2,192,384]{3,2,1,0:T(8,128)(2,1)} %broadcast_in_dim.21), calls=%async_computation.1 | async-start | bytes 2359296 | tf_op jit(solution)/shard_map/all_to_all | solution.py:119
  35.4 150.5 %all-gather.9.cloned.1.call-start = ((), (), s32[]{:S(2)}) async-start(), calls=%async_computation.9 | async-start | bytes 5308416 | tf_op jit(solution)/shard_map/all_gather | solution.py:442
  72.7 113.2 %copy-start.41 = (f32[2,768]{1,0:T(2,128)}, f32[2,768]{1,0:T(2,128)S(1)}, u32[]{:S(2)}) copy-start(f32[2,768]{1,0:T(2,128)S(1)} %get-tuple-element.282.shift_ref) | copy-start | bytes 18436
  72.7 113.2 %copy-start.42 = (f32[2,768]{1,0:T(2,128)}, f32[2,768]{1,0:T(2,128)S(1)}, u32[]{:S(2)}) copy-start(f32[2,768]{1,0:T(2,128)S(1)} %get-tuple-element.329.gain_ref) | copy-start | bytes 18436
  72.7 212.3 %copy-start.43 = (f32[2,768]{1,0:T(2,128)}, f32[2,768]{1,0:T(2,128)S(1)}, u32[]{:S(2)}) copy-start(f32[2,768]{1,0:T(2,128)S(1)} %get-tuple-element.280.shift_ref) | copy-start | bytes 18436
  72.7 212.3 %copy-start.44 = (f32[2,768]{1,0:T(2,128)}, f32[2,768]{1,0:T(2,128)S(1)}, u32[]{:S(2)}) copy-start(f32[2,768]{1,0:T(2,128)S(1)} %get-tuple-element.331.gain_ref) | copy-start | bytes 18436
  99.6 86.1 %copy-start.5 = (f32[2,208,768]{2,1,0:T(8,128)}, f32[2,208,768]{2,1,0:T(8,128)S(1)}, u32[]{:S(2)}) copy-start(f32[2,208,768]{2,1,0:T(8,128)S(1)} %get-tuple-element.96.mid_ref) | copy-start | bytes 3833860
  99.7 185.3 %all-gather.11.cloned.1.call-start = ((), (), s32[]{:S(2)}) async-start(), calls=%async_computation.10 | async-start | bytes 5308416 | tf_op jit(solution)/shard_map/all_gather | solution.py:442
  102.1 51.5 %collective-permute-start = (bf16[264,768]{1,0:T(8,128)(2,1)S(1)}, bf16[264,768]{1,0:T(8,128)(2,1)S(1)}, u32[]{:S(2)}, u32[]{:S(2)}) collective-permute-start(bf16[264,768]{1,0:T(8,128)(2,1)S(1)} %convolution_convert_fusion.10), channel_id=1, source_target_pairs={{0,1},{1,0},{2,3},{3,2},{4,5},{5,4},{6,7},{7,6},{8,9},{9,8},{10,11... | collective-permute-start | bytes 1216520 | tf_op jit(solution)/shard_map/ppermute | solution.py:29
  104.1 30.6 %collective-permute-start.2 = (bf16[264,768]{1,0:T(8,128)(2,1)S(1)}, bf16[264,768]{1,0:T(8,128)(2,1)S(1)}, u32[]{:S(2)}, u32[]{:S(2)}) collective-permute-start(bf16[264,768]{1,0:T(8,128)(2,1)S(1)} %convolution_convert_fusion.9), channel_id=1, source_target_pairs={{0,2},{1,3},{2,0},{3,1},{4,6},{5,7},{6,4},{7,5},{8,10},{9,11},{10,... | collective-permute-start | bytes 1216520 | tf_op jit(solution)/shard_map/ppermute | solution.py:29
  108.0 26.8 %collective-permute-start.3 = (bf16[264,768]{1,0:T(8,128)(2,1)S(1)}, bf16[264,768]{1,0:T(8,128)(2,1)S(1)}, u32[]{:S(2)}, u32[]{:S(2)}) collective-permute-start(bf16[264,768]{1,0:T(8,128)(2,1)S(1)} %convolution_convert_fusion.8), channel_id=1, source_target_pairs={{0,3},{1,2},{2,1},{3,0},{4,7},{5,6},{6,5},{7,4},{8,11},{9,10},{10,... | collective-permute-start | bytes 1216520 | tf_op jit(solution)/shard_map/ppermute | solution.py:29
  110.2 73.8 %copy-start.134 = (f32[416]{0:T(512)}, f32[416]{0:T(512)S(1)}, u32[]{:S(2)}) copy-start(f32[416]{0:T(512)S(1)} %get-tuple-element.228) | copy-start | bytes 4996
  146.2 35.5 %collective-permute-start.5 = (bf16[264,768]{1,0:T(8,128)(2,1)S(1)}, bf16[264,768]{1,0:T(8,128)(2,1)S(1)}, u32[]{:S(2)}, u32[]{:S(2)}) collective-permute-start(bf16[264,768]{1,0:T(8,128)(2,1)S(1)} %get-tuple-element.268), channel_id=1, source_target_pairs={{0,3},{1,2},{2,1},{3,0},{4,7},{5,6},{6,5},{7,4},{8,11},{9,10},{10,... | collective-permute-start | bytes 1216520 | tf_op jit(solution)/shard_map/ppermute | solution.py:29
  148.1 33.6 %collective-permute-start.4 = (bf16[264,768]{1,0:T(8,128)(2,1)S(1)}, bf16[264,768]{1,0:T(8,128)(2,1)S(1)}, u32[]{:S(2)}, u32[]{:S(2)}) collective-permute-start(bf16[264,768]{1,0:T(8,128)(2,1)S(1)} %get-tuple-element.269), channel_id=1, source_target_pairs={{0,2},{1,3},{2,0},{3,1},{4,6},{5,7},{6,4},{7,5},{8,10},{9,11},{10,... | collective-permute-start | bytes 1216520 | tf_op jit(solution)/shard_map/ppermute | solution.py:29
  162.9 20.4 %collective-permute-start.1 = (bf16[264,768]{1,0:T(8,128)(2,1)S(1)}, bf16[264,768]{1,0:T(8,128)(2,1)S(1)}, u32[]{:S(2)}, u32[]{:S(2)}) collective-permute-start(bf16[264,768]{1,0:T(8,128)(2,1)S(1)} %get-tuple-element.267), channel_id=1, source_target_pairs={{0,1},{1,0},{2,3},{3,2},{4,5},{5,4},{6,7},{7,6},{8,9},{9,8},{10,11... | collective-permute-start | bytes 1216520 | tf_op jit(solution)/shard_map/ppermute | solution.py:29
  199.5 85.3 %copy-start.6 = (f32[2,208,768]{2,1,0:T(8,128)}, f32[2,208,768]{2,1,0:T(8,128)S(1)}, u32[]{:S(2)}) copy-start(f32[2,208,768]{2,1,0:T(8,128)S(1)} %get-tuple-element.118.mid_ref) | copy-start | bytes 3833860
  199.5 480.3 %reduce-scatter.4.cloned.1.call-start = ((), (), s32[]{:S(2)}) async-start(), calls=%async_computation.6 | async-start | bytes 15925248 | tf_op jit(solution)/shard_map/reduce_scatter | solution.py:364
  201.4 28.6 %collective-permute-start.8 = (bf16[264,768]{1,0:T(8,128)(2,1)S(1)}, bf16[264,768]{1,0:T(8,128)(2,1)S(1)}, u32[]{:S(2)}, u32[]{:S(2)}) collective-permute-start(bf16[264,768]{1,0:T(8,128)(2,1)S(1)} %convolution_convert_fusion.5), channel_id=1, source_target_pairs={{0,2},{1,3},{2,0},{3,1},{4,6},{5,7},{6,4},{7,5},{8,10},{9,11},{10,... | collective-permute-start | bytes 1216520 | tf_op jit(solution)/shard_map/ppermute | solution.py:29
  202.9 27.2 %collective-permute-start.9 = (bf16[264,768]{1,0:T(8,128)(2,1)S(1)}, bf16[264,768]{1,0:T(8,128)(2,1)S(1)}, u32[]{:S(2)}, u32[]{:S(2)}) collective-permute-start(bf16[264,768]{1,0:T(8,128)(2,1)S(1)} %convolution_convert_fusion.4), channel_id=1, source_target_pairs={{0,3},{1,2},{2,1},{3,0},{4,7},{5,6},{6,5},{7,4},{8,11},{9,10},{10,... | collective-permute-start | bytes 1216520 | tf_op jit(solution)/shard_map/ppermute | solution.py:29
  207.0 44.9 %collective-permute-start.6 = (bf16[264,768]{1,0:T(8,128)(2,1)S(1)}, bf16[264,768]{1,0:T(8,128)(2,1)S(1)}, u32[]{:S(2)}, u32[]{:S(2)}) collective-permute-start(bf16[264,768]{1,0:T(8,128)(2,1)S(1)} %convolution_convert_fusion.6), channel_id=1, source_target_pairs={{0,1},{1,0},{2,3},{3,2},{4,5},{5,4},{6,7},{7,6},{8,9},{9,8},{10,11... | collective-permute-start | bytes 1216520 | tf_op jit(solution)/shard_map/ppermute | solution.py:29
  241.5 39.3 %collective-permute-start.11 = (bf16[264,768]{1,0:T(8,128)(2,1)S(1)}, bf16[264,768]{1,0:T(8,128)(2,1)S(1)}, u32[]{:S(2)}, u32[]{:S(2)}) collective-permute-start(bf16[264,768]{1,0:T(8,128)(2,1)S(1)} %get-tuple-element.264), channel_id=1, source_target_pairs={{0,3},{1,2},{2,1},{3,0},{4,7},{5,6},{6,5},{7,4},{8,11},{9,10},{10,... | collective-permute-start | bytes 1216520 | tf_op jit(solution)/shard_map/ppermute | solution.py:29
  243.7 37.1 %collective-permute-start.10 = (bf16[264,768]{1,0:T(8,128)(2,1)S(1)}, bf16[264,768]{1,0:T(8,128)(2,1)S(1)}, u32[]{:S(2)}, u32[]{:S(2)}) collective-permute-start(bf16[264,768]{1,0:T(8,128)(2,1)S(1)} %get-tuple-element.265), channel_id=1, source_target_pairs={{0,2},{1,3},{2,0},{3,1},{4,6},{5,7},{6,4},{7,5},{8,10},{9,11},{10,... | collective-permute-start | bytes 1216520 | tf_op jit(solution)/shard_map/ppermute | solution.py:29
  261.3 21.0 %collective-permute-start.7 = (bf16[264,768]{1,0:T(8,128)(2,1)S(1)}, bf16[264,768]{1,0:T(8,128)(2,1)S(1)}, u32[]{:S(2)}, u32[]{:S(2)}) collective-permute-start(bf16[264,768]{1,0:T(8,128)(2,1)S(1)} %get-tuple-element.263), channel_id=1, source_target_pairs={{0,1},{1,0},{2,3},{3,2},{4,5},{5,4},{6,7},{7,6},{8,9},{9,8},{10,11... | collective-permute-start | bytes 1216520 | tf_op jit(solution)/shard_map/ppermute | solution.py:29
  298.0 29.0 %collective-permute-start.14 = (bf16[264,768]{1,0:T(8,128)(2,1)S(1)}, bf16[264,768]{1,0:T(8,128)(2,1)S(1)}, u32[]{:S(2)}, u32[]{:S(2)}) collective-permute-start(bf16[264,768]{1,0:T(8,128)(2,1)S(1)} %convolution_convert_fusion.1), channel_id=1, source_target_pairs={{0,2},{1,3},{2,0},{3,1},{4,6},{5,7},{6,4},{7,5},{8,10},{9,11},{10,... | collective-permute-start | bytes 1216520 | tf_op jit(solution)/shard_map/ppermute | solution.py:29
  298.2 28.8 %collective-permute-start.15 = (bf16[264,768]{1,0:T(8,128)(2,1)S(1)}, bf16[264,768]{1,0:T(8,128)(2,1)S(1)}, u32[]{:S(2)}, u32[]{:S(2)}) collective-permute-start(bf16[264,768]{1,0:T(8,128)(2,1)S(1)} %convolution_convert_fusion), channel_id=1, source_target_pairs={{0,3},{1,2},{2,1},{3,0},{4,7},{5,6},{6,5},{7,4},{8,11},{9,10},{10,... | collective-permute-start | bytes 1216520 | tf_op jit(solution)/shard_map/ppermute | solution.py:29
  300.4 46.8 %collective-permute-start.12 = (bf16[264,768]{1,0:T(8,128)(2,1)S(1)}, bf16[264,768]{1,0:T(8,128)(2,1)S(1)}, u32[]{:S(2)}, u32[]{:S(2)}) collective-permute-start(bf16[264,768]{1,0:T(8,128)(2,1)S(1)} %convolution_convert_fusion.2), channel_id=1, source_target_pairs={{0,1},{1,0},{2,3},{3,2},{4,5},{5,4},{6,7},{7,6},{8,9},{9,8},{10,11... | collective-permute-start | bytes 1216520 | tf_op jit(solution)/shard_map/ppermute | solution.py:29
  337.5 37.3 %collective-permute-start.16 = (bf16[264,768]{1,0:T(8,128)(2,1)S(1)}, bf16[264,768]{1,0:T(8,128)(2,1)S(1)}, u32[]{:S(2)}, u32[]{:S(2)}) collective-permute-start(bf16[264,768]{1,0:T(8,128)(2,1)S(1)} %get-tuple-element.261), channel_id=1, source_target_pairs={{0,2},{1,3},{2,0},{3,1},{4,6},{5,7},{6,4},{7,5},{8,10},{9,11},{10,... | collective-permute-start | bytes 1216520 | tf_op jit(solution)/shard_map/ppermute | solution.py:29
  356.4 18.4 %collective-permute-start.17 = (bf16[264,768]{1,0:T(8,128)(2,1)S(1)}, bf16[264,768]{1,0:T(8,128)(2,1)S(1)}, u32[]{:S(2)}, u32[]{:S(2)}) collective-permute-start(bf16[264,768]{1,0:T(8,128)(2,1)S(1)} %get-tuple-element.260), channel_id=1, source_target_pairs={{0,3},{1,2},{2,1},{3,0},{4,7},{5,6},{6,5},{7,4},{8,11},{9,10},{10,... | collective-permute-start | bytes 1216520 | tf_op jit(solution)/shard_map/ppermute | solution.py:29
  358.5 24.3 %collective-permute-start.13 = (bf16[264,768]{1,0:T(8,128)(2,1)S(1)}, bf16[264,768]{1,0:T(8,128)(2,1)S(1)}, u32[]{:S(2)}, u32[]{:S(2)}) collective-permute-start(bf16[264,768]{1,0:T(8,128)(2,1)S(1)} %get-tuple-element.259), channel_id=1, source_target_pairs={{0,1},{1,0},{2,3},{3,2},{4,5},{5,4},{6,7},{7,6},{8,9},{9,8},{10,11... | collective-permute-start | bytes 1216520 | tf_op jit(solution)/shard_map/ppermute | solution.py:29
  388.6 38.5 %collective-permute-start.21 = (bf16[264,768]{1,0:T(8,128)(2,1)S(1)}, bf16[264,768]{1,0:T(8,128)(2,1)S(1)}, u32[]{:S(2)}, u32[]{:S(2)}) collective-permute-start(bf16[264,768]{1,0:T(8,128)(2,1)S(1)} %fusion.149), channel_id=1, source_target_pairs={{0,3},{1,2},{2,1},{3,0},{4,7},{5,6},{6,5},{7,4},{8,11},{9,10},{10,... | collective-permute-start | bytes 1216520 | tf_op jit(solution)/shard_map/ppermute | solution.py:29
  391.0 36.1 %collective-permute-start.20 = (bf16[264,768]{1,0:T(8,128)(2,1)S(1)}, bf16[264,768]{1,0:T(8,128)(2,1)S(1)}, u32[]{:S(2)}, u32[]{:S(2)}) collective-permute-start(bf16[264,768]{1,0:T(8,128)(2,1)S(1)} %fusion.148), channel_id=1, source_target_pairs={{0,2},{1,3},{2,0},{3,1},{4,6},{5,7},{6,4},{7,5},{8,10},{9,11},{10,... | collective-permute-start | bytes 1216520 | tf_op jit(solution)/shard_map/ppermute | solution.py:29
  393.5 45.9 %collective-permute-start.18 = (bf16[264,768]{1,0:T(8,128)(2,1)S(1)}, bf16[264,768]{1,0:T(8,128)(2,1)S(1)}, u32[]{:S(2)}, u32[]{:S(2)}) collective-permute-start(bf16[264,768]{1,0:T(8,128)(2,1)S(1)} %fusion.147), channel_id=1, source_target_pairs={{0,1},{1,0},{2,3},{3,2},{4,5},{5,4},{6,7},{7,6},{8,9},{9,8},{10,11... | collective-permute-start | bytes 1216520 | tf_op jit(solution)/shard_map/ppermute | solution.py:29
  437.3 28.2 %collective-permute-start.22 = (bf16[264,768]{1,0:T(8,128)(2,1)S(1)}, bf16[264,768]{1,0:T(8,128)(2,1)S(1)}, u32[]{:S(2)}, u32[]{:S(2)}) collective-permute-start(bf16[264,768]{1,0:T(8,128)(2,1)S(1)} %get-tuple-element.256), channel_id=1, source_target_pairs={{0,2},{1,3},{2,0},{3,1},{4,6},{5,7},{6,4},{7,5},{8,10},{9,11},{10,... | collective-permute-start | bytes 1216520 | tf_op jit(solution)/shard_map/ppermute | solution.py:29
  437.4 28.2 %collective-permute-start.23 = (bf16[264,768]{1,0:T(8,128)(2,1)S(1)}, bf16[264,768]{1,0:T(8,128)(2,1)S(1)}, u32[]{:S(2)}, u32[]{:S(2)}) collective-permute-start(bf16[264,768]{1,0:T(8,128)(2,1)S(1)} %get-tuple-element.257), channel_id=1, source_target_pairs={{0,3},{1,2},{2,1},{3,0},{4,7},{5,6},{6,5},{7,4},{8,11},{9,10},{10,... | collective-permute-start | bytes 1216520 | tf_op jit(solution)/shard_map/ppermute | solution.py:29
  449.1 25.1 %collective-permute-start.19 = (bf16[264,768]{1,0:T(8,128)(2,1)S(1)}, bf16[264,768]{1,0:T(8,128)(2,1)S(1)}, u32[]{:S(2)}, u32[]{:S(2)}) collective-permute-start(bf16[264,768]{1,0:T(8,128)(2,1)S(1)} %get-tuple-element.255), channel_id=1, source_target_pairs={{0,1},{1,0},{2,3},{3,2},{4,5},{5,4},{6,7},{7,6},{8,9},{9,8},{10,11... | collective-permute-start | bytes 1216520 | tf_op jit(solution)/shard_map/ppermute | solution.py:29
  511.9 21.5 %collective-permute-start.24 = (bf16[264,768]{1,0:T(8,128)(2,1)}, bf16[264,768]{1,0:T(8,128)(2,1)}, u32[]{:S(2)}, u32[]{:S(2)}) collective-permute-start(bf16[264,768]{1,0:T(8,128)(2,1)} %fusion.151), channel_id=1, source_target_pairs={{0,1},{1,0},{2,3},{3,2},{4,5},{5,4},{6,7},{7,6},{8,9},{9,8},{10,11... | collective-permute-start | bytes 1216520 | tf_op jit(solution)/shard_map/ppermute | solution.py:29
  534.6 299.0 %reduce-scatter.6.cloned.1.call-start = ((), (), s32[]{:S(2)}) async-start(), calls=%async_computation.7 | async-start | bytes 15925248 | tf_op jit(solution)/shard_map/reduce_scatter | solution.py:364
  534.6 29.8 %collective-permute-start.26 = (bf16[264,768]{1,0:T(8,128)(2,1)}, bf16[264,768]{1,0:T(8,128)(2,1)S(1)}, u32[]{:S(2)}, u32[]{:S(2)}) collective-permute-start(bf16[264,768]{1,0:T(8,128)(2,1)} %fusion.152), channel_id=1, source_target_pairs={{0,2},{1,3},{2,0},{3,1},{4,6},{5,7},{6,4},{7,5},{8,10},{9,11},{10,... | collective-permute-start | bytes 1216520 | tf_op jit(solution)/shard_map/ppermute | solution.py:29
  536.9 27.6 %collective-permute-start.27 = (bf16[264,768]{1,0:T(8,128)(2,1)}, bf16[264,768]{1,0:T(8,128)(2,1)S(1)}, u32[]{:S(2)}, u32[]{:S(2)}) collective-permute-start(bf16[264,768]{1,0:T(8,128)(2,1)} %fusion.153), channel_id=1, source_target_pairs={{0,3},{1,2},{2,1},{3,0},{4,7},{5,6},{6,5},{7,4},{8,11},{9,10},{10,... | collective-permute-start | bytes 1216520 | tf_op jit(solution)/shard_map/ppermute | solution.py:29
  575.6 36.5 %collective-permute-start.28 = (bf16[264,768]{1,0:T(8,128)(2,1)S(1)}, bf16[264,768]{1,0:T(8,128)(2,1)S(1)}, u32[]{:S(2)}, u32[]{:S(2)}) collective-permute-start(bf16[264,768]{1,0:T(8,128)(2,1)S(1)} %get-tuple-element.252), channel_id=1, source_target_pairs={{0,2},{1,3},{2,0},{3,1},{4,6},{5,7},{6,4},{7,5},{8,10},{9,11},{10,... | collective-permute-start | bytes 1216520 | tf_op jit(solution)/shard_map/ppermute | solution.py:29
  584.4 27.7 %collective-permute-start.29 = (bf16[264,768]{1,0:T(8,128)(2,1)S(1)}, bf16[264,768]{1,0:T(8,128)(2,1)S(1)}, u32[]{:S(2)}, u32[]{:S(2)}) collective-permute-start(bf16[264,768]{1,0:T(8,128)(2,1)S(1)} %get-tuple-element.253), channel_id=1, source_target_pairs={{0,3},{1,2},{2,1},{3,0},{4,7},{5,6},{6,5},{7,4},{8,11},{9,10},{10,... | collective-permute-start | bytes 1216520 | tf_op jit(solution)/shard_map/ppermute | solution.py:29
  596.6 23.8 %collective-permute-start.25 = (bf16[264,768]{1,0:T(8,128)(2,1)S(1)}, bf16[264,768]{1,0:T(8,128)(2,1)S(1)}, u32[]{:S(2)}, u32[]{:S(2)}) collective-permute-start(bf16[264,768]{1,0:T(8,128)(2,1)S(1)} %get-tuple-element.251), channel_id=1, source_target_pairs={{0,1},{1,0},{2,3},{3,2},{4,5},{5,4},{6,7},{7,6},{8,9},{9,8},{10,11... | collective-permute-start | bytes 1216520 | tf_op jit(solution)/shard_map/ppermute | solution.py:29
  653.7 25.1 %collective-permute-start.30 = (bf16[264,768]{1,0:T(8,128)(2,1)}, bf16[264,768]{1,0:T(8,128)(2,1)}, u32[]{:S(2)}, u32[]{:S(2)}) collective-permute-start(bf16[264,768]{1,0:T(8,128)(2,1)} %fusion.155), channel_id=1, source_target_pairs={{0,1},{1,0},{2,3},{3,2},{4,5},{5,4},{6,7},{7,6},{8,9},{9,8},{10,11... | collective-permute-start | bytes 1216520 | tf_op jit(solution)/shard_map/ppermute | solution.py:29
  679.9 237.4 %reduce-scatter.8.cloned.1.call-start = ((), (), s32[]{:S(2)}) async-start(), calls=%async_computation.8 | async-start | bytes 10616832 | tf_op jit(solution)/shard_map/reduce_scatter | solution.py:364
  686.6 37.8 %collective-permute-start.33 = (bf16[264,768]{1,0:T(8,128)(2,1)}, bf16[264,768]{1,0:T(8,128)(2,1)S(1)}, u32[]{:S(2)}, u32[]{:S(2)}) collective-permute-start(bf16[264,768]{1,0:T(8,128)(2,1)} %fusion.157), channel_id=1, source_target_pairs={{0,3},{1,2},{2,1},{3,0},{4,7},{5,6},{6,5},{7,4},{8,11},{9,10},{10,... | collective-permute-start | bytes 1216520 | tf_op jit(solution)/shard_map/ppermute | solution.py:29
  688.7 35.7 %collective-permute-start.32 = (bf16[264,768]{1,0:T(8,128)(2,1)}, bf16[264,768]{1,0:T(8,128)(2,1)S(1)}, u32[]{:S(2)}, u32[]{:S(2)}) collective-permute-start(bf16[264,768]{1,0:T(8,128)(2,1)} %fusion.156), channel_id=1, source_target_pairs={{0,2},{1,3},{2,0},{3,1},{4,6},{5,7},{6,4},{7,5},{8,10},{9,11},{10,... | collective-permute-start | bytes 1216520 | tf_op jit(solution)/shard_map/ppermute | solution.py:29
  735.9 28.4 %collective-permute-start.34 = (bf16[264,768]{1,0:T(8,128)(2,1)}, bf16[264,768]{1,0:T(8,128)(2,1)}, u32[]{:S(2)}, u32[]{:S(2)}) collective-permute-start(bf16[264,768]{1,0:T(8,128)(2,1)} %get-tuple-element.248), channel_id=1, source_target_pairs={{0,2},{1,3},{2,0},{3,1},{4,6},{5,7},{6,4},{7,5},{8,10},{9,11},{10,... | collective-permute-start | bytes 1216520 | tf_op jit(solution)/shard_map/ppermute | solution.py:29
  735.9 28.4 %collective-permute-start.35 = (bf16[264,768]{1,0:T(8,128)(2,1)}, bf16[264,768]{1,0:T(8,128)(2,1)}, u32[]{:S(2)}, u32[]{:S(2)}) collective-permute-start(bf16[264,768]{1,0:T(8,128)(2,1)} %get-tuple-element.249), channel_id=1, source_target_pairs={{0,3},{1,2},{2,1},{3,0},{4,7},{5,6},{6,5},{7,4},{8,11},{9,10},{10,... | collective-permute-start | bytes 1216520 | tf_op jit(solution)/shard_map/ppermute | solution.py:29
  747.6 42.8 %collective-permute-start.31 = (bf16[264,768]{1,0:T(8,128)(2,1)}, bf16[264,768]{1,0:T(8,128)(2,1)}, u32[]{:S(2)}, u32[]{:S(2)}) collective-permute-start(bf16[264,768]{1,0:T(8,128)(2,1)} %get-tuple-element.247), channel_id=1, source_target_pairs={{0,1},{1,0},{2,3},{3,2},{4,5},{5,4},{6,7},{7,6},{8,9},{9,8},{10,11... | collective-permute-start | bytes 1216520 | tf_op jit(solution)/shard_map/ppermute | solution.py:29
  825.6 4.9 collective-permute-start.36
  834.8 15.5 %collective-permute-start.37 = (bf16[1,2,4,96,384]{4,3,2,1,0:T(8,128)(2,1)S(1)}, bf16[1,2,4,96,384]{4,3,2,1,0:T(8,128)(2,1)}, u32[]{:S(2)}, u32[]{:S(2)}) collective-permute-start(bf16[1,2,4,96,384]{4,3,2,1,0:T(8,128)(2,1)S(1)} %dynamic-slice_bitcast_fusion.3), channel_id=1, source_target_pairs={{0,8},{4,12},{8,0},{12,4},{16,24},{20,28},{24,16},{28,20},{1,9},{5... | collective-permute-start | bytes 1769480 | tf_op jit(solution)/shard_map/ppermute | solution.py:29
  837.6 16.4 %collective-permute-start.39 = (bf16[1,2,4,104,384]{4,3,2,1,0:T(8,128)(2,1)S(1)}, bf16[1,2,4,104,384]{4,3,2,1,0:T(8,128)(2,1)S(1)}, u32[]{:S(2)}, u32[]{:S(2)}) collective-permute-start(bf16[1,2,4,104,384]{4,3,2,1,0:T(8,128)(2,1)S(1)} %dynamic-slice_bitcast_fusion), channel_id=1, source_target_pairs={{0,16},{4,20},{8,24},{12,28},{16,0},{20,4},{24,8},{28,12},{1,17},{... | collective-permute-start | bytes 1916936 | tf_op jit(solution)/shard_map/ppermute | solution.py:29
  851.7 12.8 %collective-permute-start.38 = (bf16[1,1,4,96,384]{4,3,2,1,0:T(8,128)(2,1)S(1)}, bf16[1,1,4,96,384]{4,3,2,1,0:T(8,128)(2,1)S(1)}, u32[]{:S(2)}, u32[]{:S(2)}) collective-permute-start(bf16[1,1,4,96,384]{4,3,2,1,0:T(8,128)(2,1)S(1)} %constant_dynamic-slice_fusion.3), channel_id=1, source_target_pairs={{0,16},{4,20},{8,24},{12,28},{16,0},{20,4},{24,8},{28,12},{1,17},{... | collective-permute-start | bytes 884744 | tf_op jit(solution)/shard_map/ppermute | solution.py:29
  854.3 10.4 %collective-permute-start.40 = (bf16[1,1,4,104,384]{4,3,2,1,0:T(8,128)(2,1)S(1)}, bf16[1,1,4,104,384]{4,3,2,1,0:T(8,128)(2,1)S(1)}, u32[]{:S(2)}, u32[]{:S(2)}) collective-permute-start(bf16[1,1,4,104,384]{4,3,2,1,0:T(8,128)(2,1)S(1)} %constant_dynamic-slice_fusion.2), channel_id=1, source_target_pairs={{0,8},{4,12},{8,0},{12,4},{16,24},{20,28},{24,16},{28,20},{1,9},{5... | collective-permute-start | bytes 958472 | tf_op jit(solution)/shard_map/ppermute | solution.py:29
  855.0 34.4 %collective-permute-start.43 = (bf16[2,192,768]{2,1,0:T(8,128)(2,1)S(1)}, bf16[2,192,768]{2,1,0:T(8,128)(2,1)S(1)}, u32[]{:S(2)}, u32[]{:S(2)}) collective-permute-start(bf16[2,192,768]{2,1,0:T(8,128)(2,1)S(1)} %get-tuple-element.239), channel_id=1, source_target_pairs={{0,2},{1,3},{2,0},{3,1},{4,6},{5,7},{6,4},{7,5},{8,10},{9,11},{10,... | collective-permute-start | bytes 1769480 | tf_op jit(solution)/shard_map/ppermute | solution.py:29
  889.6 13.1 %collective-permute-start.44 = (bf16[1,192,768]{2,1,0:T(8,128)(2,1)S(1)}, bf16[1,192,768]{2,1,0:T(8,128)(2,1)S(1)}, u32[]{:S(2)}, u32[]{:S(2)}) collective-permute-start(bf16[1,192,768]{2,1,0:T(8,128)(2,1)S(1)} %get-tuple-element.275), channel_id=1, source_target_pairs={{0,1},{1,0},{2,3},{3,2},{4,5},{5,4},{6,7},{7,6},{8,9},{9,8},{10,11... | collective-permute-start | bytes 884744 | tf_op jit(solution)/shard_map/ppermute | solution.py:29
  889.7 15.0 %collective-permute-start.41 = (bf16[2,200,384]{2,1,0:T(8,128)(2,1)S(1)}, bf16[2,200,384]{2,1,0:T(8,128)(2,1)S(1)}, u32[]{:S(2)}, u32[]{:S(2)}) collective-permute-start(bf16[2,200,384]{2,1,0:T(8,128)(2,1)S(1)} %fusion.194), channel_id=1, source_target_pairs={{0,2},{1,3},{2,0},{3,1},{4,6},{5,7},{6,4},{7,5},{8,10},{9,11},{10,... | collective-permute-start | bytes 921608 | tf_op jit(solution)/shard_map/ppermute | solution.py:29
  904.9 5.3 collective-permute-start.42
  922.1 7.1 collective-permute-start.45
  923.7 7.2 collective-permute-start.47
  929.3 10.9 %collective-permute-start.46 = (bf16[1,2,288,384]{3,2,1,0:T(8,128)(2,1)S(1)}, bf16[1,2,288,384]{3,2,1,0:T(8,128)(2,1)S(1)}, u32[]{:S(2)}, u32[]{:S(2)}) collective-permute-start(bf16[1,2,288,384]{3,2,1,0:T(8,128)(2,1)S(1)} %fusion.208), channel_id=1, source_target_pairs={{0,8},{4,12},{8,0},{12,4},{16,24},{20,28},{24,16},{28,20},{1,9},{5... | collective-permute-start | bytes 1327112 | tf_op jit(solution)/shard_map/ppermute | solution.py:29
  930.9 10.9 %collective-permute-start.48 = (bf16[1,2,296,384]{3,2,1,0:T(8,128)(2,1)S(1)}, bf16[1,2,296,384]{3,2,1,0:T(8,128)(2,1)S(1)}, u32[]{:S(2)}, u32[]{:S(2)}) collective-permute-start(bf16[1,2,296,384]{3,2,1,0:T(8,128)(2,1)S(1)} %fusion.207), channel_id=1, source_target_pairs={{0,16},{4,20},{8,24},{12,28},{16,0},{20,4},{24,8},{28,12},{1,17},{... | collective-permute-start | bytes 1363976 | tf_op jit(solution)/shard_map/ppermute | solution.py:29
  942.3 3.8 collective-permute-start.49
  (161 other events, 2060.0 us)
Sparse Core Ops, SparseCore 0:
  30.8 37.8 all-gather.6
  99.8 38.8 all-gather.8
  199.6 38.0 all-gather.10
  534.7 100.8 reduce-scatter.3
  680.0 101.0 reduce-scatter.5
  833.7 83.5 reduce-scatter.7
